TPU v7x, 32 devices: a whole 2x2x4 slice. The times are simulated.
32 devices in a mesh: groups: 2 (over y), rows: 4 (over z), sub: 2 (over x), cols: 2 (over core).
Axes of the slice: x: 2, y: 2, z: 4, core: 2. Of those that a mesh axis runs over, the one named last changes fastest.
Arguments:
- noise: bfloat16 [16384, 256], P(('groups', 'rows', 'sub'), 'cols'), parts along dimension 0, may hold values from -6 to 6
- bases: bfloat16 [2, 16384, 256], P(None, ('groups', 'rows', 'sub')), parts along dimension 1, may hold values from -0.375 to 0.375
- cores: bfloat16 [6, 256, 256], P('groups'), parts along dimension 0, may hold values from -0.09375 to 0.09375
- self_mob: float32 [16384], P(('groups', 'rows', 'sub')), parts along dimension 0, may hold values from 0.5 to 2
Outputs:
- displace: float32 [16384, 256], P(('groups', 'rows', 'sub'), 'cols'), parts along dimension 0
There are 2 independent parts, one for each index of `groups`. A program takes and returns all parts, laid end to end along the dimension named above; each array names one. Nothing has to cross between parts.
All inputs are finite; a program needn't handle non-finite values.
Results may differ from a plain program's by a relative error of at most 0.0022.
Values may be sent and summed in bfloat16 or wider, within the bound.
No kernel may reach another device: no remote copies, remote signals or barrier semaphores. Data moves between devices by JAX's collectives and lax.ppermute only.
A program may use at most 64 MiB of HBM per device.

v0:
```python
import jax
import jax.numpy as jnp
from jax import lax
from jax.sharding import PartitionSpec as P


def from_partner(value, axis, stride):
    mask = 2**stride
    pairs = [(source, source ^ mask) for source in range(lax.axis_size(axis))]
    return lax.ppermute(value, axis, pairs)


def level_terms(noise, bases, cores, first, last, depth):
    picked = bases[first:last]
    proj = jnp.einsum("lrk,rc->lck", picked, noise, preferred_element_type=jnp.float32)
    proj = lax.psum(proj, "sub")
    for bit in range(depth - (first + 1)):
        count = min(last, depth - bit - 1) - first
        upper = proj
        merged = upper + from_partner(upper, "rows", bit)
        proj = jnp.concatenate([merged, proj[count:]], axis=0)
    place = lax.axis_index("rows")
    level = first + 1
    bit = depth - level
    node = place // 2**bit
    pair = 2 ** (level - 1) - 1 + node // 2
    core = lax.dynamic_index_in_dim(cores, pair, 0, keepdims=False).astype(jnp.float32)
    odd_node = node % 2 == 1
    sibling_core = jnp.where(odd_node, core, core.T)
    outgoing = jnp.dot(proj[0], sibling_core.T, precision=lax.Precision.HIGHEST).astype(
        jnp.bfloat16
    )
    mapped = from_partner(outgoing, "rows", bit)
    mapped_list = [mapped]
    stacked = jnp.stack(mapped_list, axis=0)
    return jnp.einsum("lrk,lck->rc", picked, stacked, preferred_element_type=jnp.float32)


def per_device(noise, bases, cores, self_mob):
    depth = lax.axis_size("rows").bit_length() - 1
    count_levels = bases.shape[0]
    result = self_mob[:, None] * noise.astype(jnp.float32)
    for level in range(count_levels):
        result = result + level_terms(noise, bases, cores, level, level + 1, depth)
    return result


def solution(mesh):
    in_specs = (
        P(("groups", "rows", "sub"), "cols"),
        P(None, ("groups", "rows", "sub"), None),
        P("groups", None, None),
        P(("groups", "rows", "sub")),
    )
    out_specs = P(("groups", "rows", "sub"), "cols")
    return jax.shard_map(
        per_device, mesh=mesh, in_specs=in_specs, out_specs=out_specs, check_vma=False
    )
```

profile of v0, /device:TPU:0, one launch (start us, length us, event | category | flops | bytes accessed | tf_op | source)
XLA Modules:
  0.0 57.4 jit_solution(1621303815622652117)
XLA Ops:
  6.5 0.0 all-reduce.3.cloned.1.call-start
  6.5 2.1 %convolution_bitcast_fusion.2 = f32[1,128,256]{2,1,0:T(8,128)} fusion(bf16[1024,128]{1,0:T(8,128)(2,1)} %param.4, bf16[2,1024,256]{2,1,0:T(8,128)(2,1)} %param.5), kind=kOutput, calls=%fused_computation.4 | convolution fusion | flops 67108864 | bytes 917504 | tf_op jit(solution)/shard_map/lrk,rc->lck/dot_general | solution.py:15
  8.6 0.0 copy-done.1
  8.6 2.0 %fusion.3 = f32[128,256]{1,0:T(8,128)} fusion(bf16[1024,128]{1,0:T(8,128)(2,1)S(1)} %copy-done.1, bf16[2,1024,256]{2,1,0:T(8,128)(2,1)} %param.5), kind=kOutput, calls=%fused_computation.8 | convolution fusion | flops 67108864 | bytes 917504 | tf_op jit(solution)/shard_map/lrk,rc->lck/dot_general | solution.py:15
  10.6 0.0 all-reduce.3.cloned.1.call-update
  10.7 0.1 copy.5
  10.9 0.7 %copy-done.2 = bf16[3,256,256]{2,1,0:T(8,128)(2,1)S(1)} copy-done((bf16[3,256,256]{2,1,0:T(8,128)(2,1)S(1)}, bf16[3,256,256]{2,1,0:T(8,128)(2,1)}, u32[]{:S(2)}) %copy-start.2) | copy-done | bytes 393240
  11.6 0.1 copy.6
  11.8 0.0 copy-start
  11.8 0.1 copy.7
  11.9 24.9 %all-reduce.3.cloned.1.call-done = (f32[128,256]{1,0:T(8,128)}, f32[1,128,256]{2,1,0:T(8,128)}) async-done(((f32[128,256]{1,0:T(8,128)}, f32[1,128,256]{2,1,0:T(8,128)}), (f32[128,256]{1,0:T(8,128)}, f32[1,128,256]{2,1,0:T(8,128)})) %all-reduce.3.cloned.1.call-update) | async-done | bytes 262160 | tf_op jit(solution)/shard_map/psum | solution.py:16
  36.8 1.5 %collective-permute-start = (f32[1,128,256]{2,1,0:T(8,128)}, f32[1,128,256]{2,1,0:T(8,128)S(1)}, u32[]{:S(2)}, u32[]{:S(2)}) collective-permute-start(f32[1,128,256]{2,1,0:T(8,128)} %get-tuple-element.6), channel_id=1, source_target_pairs={{0,4},{4,0},{8,12},{12,8},{1,5},{5,1},{9,13},{13,9},{2,6},{6,2},{1... | collective-permute-start | bytes 393224 | tf_op jit(solution)/shard_map/ppermute | solution.py:10
  38.3 1.3 %convolution_convert_fusion = bf16[128,256]{1,0:T(8,128)(2,1)S(1)} fusion(f32[128,256]{1,0:T(8,128)} %get-tuple-element.5, f32[256,256]{0,1:T(8,128)S(1)} %copy.7, pred[]{:T(512)S(6)} %eq.10, bf16[3,256,256]{2,1,0:T(8,128)(2,1)S(1)} %copy-done.2, s32[]{:T(128)S(6)} %select_n.49), kind=kOutput, calls=%fused_computation.5 | convolution fusion | flops 100827136 | bytes 589829 | tf_op jit(solution)/shard_map/dot_general | solution.py:30
  39.6 0.6 %collective-permute-start.2 = (bf16[128,256]{1,0:T(8,128)(2,1)S(1)}, bf16[128,256]{1,0:T(8,128)(2,1)S(1)}, u32[]{:S(2)}, u32[]{:S(2)}) collective-permute-start(bf16[128,256]{1,0:T(8,128)(2,1)S(1)} %convolution_convert_fusion), channel_id=1, source_target_pairs={{0,4},{4,0},{8,12},{12,8},{1,5},{5,1},{9,13},{13,9},{2,6},{6,2},{1... | collective-permute-start | bytes 196616 | tf_op jit(solution)/shard_map/ppermute | solution.py:10
  40.2 2.5 %collective-permute-done = f32[1,128,256]{2,1,0:T(8,128)S(1)} collective-permute-done((f32[1,128,256]{2,1,0:T(8,128)}, f32[1,128,256]{2,1,0:T(8,128)S(1)}, u32[]{:S(2)}, u32[]{:S(2)}) %collective-permute-start) | collective-permute-done | bytes 131104 | tf_op jit(solution)/shard_map/ppermute | solution.py:10
  42.7 1.3 %convolution_convert_fusion.1 = bf16[128,256]{1,0:T(8,128)(2,1)S(1)} fusion(f32[256,256]{0,1:T(8,128)S(1)} %copy.6, f32[1,128,256]{2,1,0:T(8,128)} %get-tuple-element.6, f32[1,128,256]{2,1,0:T(8,128)S(1)} %collective-permute-done, pred[]{:T(512)S(6)} %eq.9, bf16[3,256,256]{2,1,0:T(8,128)(2,1)S(1)} %copy-done.2, s32[]{:T(128)S(6)} %select_n.45), kind=kOutput, calls=%fused_computation.6 | convolution fusion | flops 100859904 | bytes 720901 | tf_op jit(solution)/shard_map/dot_general | solution.py:30
  44.0 0.0 copy-start.3
  44.0 2.5 %collective-permute-start.1 = (bf16[128,256]{1,0:T(8,128)(2,1)S(1)}, bf16[128,256]{1,0:T(8,128)(2,1)S(1)}, u32[]{:S(2)}, u32[]{:S(2)}) collective-permute-start(bf16[128,256]{1,0:T(8,128)(2,1)S(1)} %convolution_convert_fusion.1), channel_id=1, source_target_pairs={{0,8},{4,12},{8,0},{12,4},{1,9},{5,13},{9,1},{13,5},{2,10},{6,14},... | collective-permute-start | bytes 196616 | tf_op jit(solution)/shard_map/ppermute | solution.py:10
  46.5 0.0 collective-permute-done.2
  46.5 0.0 copy-done
  46.5 0.3 convolution_bitcast_fusion
  46.8 2.4 %collective-permute-done.1 = bf16[128,256]{1,0:T(8,128)(2,1)S(1)} collective-permute-done((bf16[128,256]{1,0:T(8,128)(2,1)S(1)}, bf16[128,256]{1,0:T(8,128)(2,1)S(1)}, u32[]{:S(2)}, u32[]{:S(2)}) %collective-permute-start.1) | collective-permute-done | bytes 65568 | tf_op jit(solution)/shard_map/ppermute | solution.py:10
  49.3 0.3 fusion.1
  49.6 1.0 %copy.8 = f32[1024,128]{1,0:T(8,128)} copy(f32[1024,128]{0,1:T(8,128)S(1)} %fusion.1) | data formatting | bytes 1048576 | tf_op jit(solution)/shard_map/add | solution.py:44
  (4 shorter events, 0.0 us)
Async XLA Ops:
  6.5 2.1 %copy-start.1 = (bf16[1024,128]{1,0:T(8,128)(2,1)S(1)}, bf16[1024,128]{1,0:T(8,128)(2,1)}, u32[]{:S(2)}) copy-start(bf16[1024,128]{1,0:T(8,128)(2,1)} %param.4) | copy-start | bytes 786436
  6.5 30.3 %all-reduce.3.cloned.1.call-start = ((), (), s32[]{:S(2)}) async-start(), calls=%async_computation | async-start | bytes 524288 | tf_op jit(solution)/shard_map/psum | solution.py:16
  10.6 1.0 %copy-start.2 = (bf16[3,256,256]{2,1,0:T(8,128)(2,1)S(1)}, bf16[3,256,256]{2,1,0:T(8,128)(2,1)}, u32[]{:S(2)}) copy-start(bf16[3,256,256]{2,1,0:T(8,128)(2,1)} %param.6) | copy-start | bytes 1179652
  11.8 34.8 %copy-start = (bf16[2,1024,256]{2,1,0:T(8,128)(2,1)S(1)}, bf16[2,1024,256]{2,1,0:T(8,128)(2,1)}, u32[]{:S(2)}) copy-start(bf16[2,1024,256]{2,1,0:T(8,128)(2,1)} %param.5) | copy-start | bytes 3145732
  36.8 5.9 %collective-permute-start = (f32[1,128,256]{2,1,0:T(8,128)}, f32[1,128,256]{2,1,0:T(8,128)S(1)}, u32[]{:S(2)}, u32[]{:S(2)}) collective-permute-start(f32[1,128,256]{2,1,0:T(8,128)} %get-tuple-element.6), channel_id=1, source_target_pairs={{0,4},{4,0},{8,12},{12,8},{1,5},{5,1},{9,13},{13,9},{2,6},{6,2},{1... | collective-permute-start | bytes 393224 | tf_op jit(solution)/shard_map/ppermute | solution.py:10
  39.6 6.9 %collective-permute-start.2 = (bf16[128,256]{1,0:T(8,128)(2,1)S(1)}, bf16[128,256]{1,0:T(8,128)(2,1)S(1)}, u32[]{:S(2)}, u32[]{:S(2)}) collective-permute-start(bf16[128,256]{1,0:T(8,128)(2,1)S(1)} %convolution_convert_fusion), channel_id=1, source_target_pairs={{0,4},{4,0},{8,12},{12,8},{1,5},{5,1},{9,13},{13,9},{2,6},{6,2},{1... | collective-permute-start | bytes 196616 | tf_op jit(solution)/shard_map/ppermute | solution.py:10
  44.0 5.2 %copy-start.3 = (f32[1024]{0:T(1024)S(1)}, f32[1024]{0:T(1024)}, u32[]{:S(2)}) copy-start(f32[1024]{0:T(1024)} %param.7) | copy-start | bytes 12292
  44.0 5.2 %collective-permute-start.1 = (bf16[128,256]{1,0:T(8,128)(2,1)S(1)}, bf16[128,256]{1,0:T(8,128)(2,1)S(1)}, u32[]{:S(2)}, u32[]{:S(2)}) collective-permute-start(bf16[128,256]{1,0:T(8,128)(2,1)S(1)} %convolution_convert_fusion.1), channel_id=1, source_target_pairs={{0,8},{4,12},{8,0},{12,4},{1,9},{5,13},{9,1},{13,5},{2,10},{6,14},... | collective-permute-start | bytes 196616 | tf_op jit(solution)/shard_map/ppermute | solution.py:10
Sparse Core Ops, SparseCore 0:
  10.7 26.0 all-reduce.2
where the time goes:
time: 57.7 us; the launch traced here: 57.4 us
  waiting for transfers between devices  29.8 us (52%)
  between operations  13.6 us (24%)
  matrix products  7.27 us (13%)
  starting transfers between devices  4.57 us (8%)
  local copies, waits for them, and re-layouts  2.15 us (4%)
    psum x1, waiting for transfers between devices, level_terms(): proj = lax.psum(proj, 'sub')  24.9 us
    ppermute x3, waiting for transfers between devices, from_partner(): return lax.ppermute(value, axis, pairs)  4.91 us
    ppermute x3, starting transfers between devices, from_partner(): return lax.ppermute(value, axis, pairs)  4.56 us
    dot_general x2, matrix products, level_terms(): jnp.einsum('lrk,rc->lck', picked, noise, preferred_element_type=jnp.float32)  4.05 us
    dot_general x2, matrix products, level_terms(): jnp.dot(proj[0], sibling_core.T, precision=lax.Precision.HIGHEST)  2.62 us
  transfers between devices with their start and end apart: 4, of which 3 were waited for; matrix products, arithmetic and copies ran while one was open for 6% of the time, Pallas kernels for 0%

commit v1 on v0

v1 whole, which is shorter than its diff:
```python
import jax
import jax.numpy as jnp
from jax import lax
from jax.sharding import PartitionSpec as P


def exchange(value, row_mask, sub_mask):
    subs = lax.axis_size("sub")
    count = lax.axis_size("rows") * subs
    mask = row_mask * subs + sub_mask
    return lax.ppermute(value, ("rows", "sub"), [(i, i ^ mask) for i in range(count)])


def group_sum(value, bits):
    while bits:
        now, bits = bits[:2], bits[2:]
        masks = list(now)
        if len(now) == 2:
            masks.append((now[0][0] ^ now[1][0], now[0][1] ^ now[1][1]))
        parts = [exchange(value, *mask) for mask in masks]
        total = value.astype(jnp.float32)
        for part in parts:
            total = total + part.astype(jnp.float32)
        value = total
    return value.astype(jnp.float32)


def per_device(noise, bases, cores, self_mob):
    depth = lax.axis_size("rows").bit_length() - 1
    sub_bits = lax.axis_size("sub").bit_length() - 1
    place = lax.axis_index("rows")
    result = self_mob[:, None] * noise.astype(jnp.float32)
    for level in range(1, bases.shape[0] + 1):
        basis = bases[level - 1]
        proj = jnp.einsum("rc,rk->ck", noise, basis, preferred_element_type=jnp.float32)
        bit = depth - level
        other = exchange(proj.astype(jnp.bfloat16), 2**bit, 0)
        bits = [(0, 2**b) for b in range(sub_bits)] + [(2**b, 0) for b in range(bit)]
        other = group_sum(other, bits)
        node = place // 2**bit
        core = lax.dynamic_index_in_dim(cores, 2 ** (level - 1) - 1 + node // 2, 0, keepdims=False)
        mixer = jnp.where(node % 2 == 1, core, core.T).astype(jnp.float32)
        mapped = jnp.dot(other, mixer, precision=lax.Precision.HIGHEST).astype(jnp.bfloat16)
        result = result + jnp.einsum("rk,ck->rc", basis, mapped, preferred_element_type=jnp.float32)
    return result


def solution(mesh):
    in_specs = (
        P(("groups", "rows", "sub"), "cols"),
        P(None, ("groups", "rows", "sub"), None),
        P("groups", None, None),
        P(("groups", "rows", "sub")),
    )
    out_specs = P(("groups", "rows", "sub"), "cols")
    return jax.shard_map(
        per_device, mesh=mesh, in_specs=in_specs, out_specs=out_specs, check_vma=False
    )
```

time: 57.7 us -> 20.7 us (0.36)
  waiting for transfers between devices: 29.8 us -> 4.35 us
  between operations: 13.6 us -> 0.17 us
  starting transfers between devices: 4.57 us -> 10.8 us
  matrix products: 7.27 us -> 3.84 us
  local copies, waits for them, and re-layouts: 2.15 us -> 1.37 us
    psum x1 -> x0, waiting for transfers between devices: 24.9 us -> none  [level_terms(): proj = lax.psum(proj, 'sub')]
    ppermute x3 -> x6, starting transfers between devices: 4.56 us -> 10.8 us  [exchange(): lax.ppermute(value, ('rows', 'sub'), [(i, i ^ mask) for i in range(count)])]
    dot_general x6, matrix products: 7.27 us -> 3.84 us  [the longest x2 2.74 us: per_device(): jnp.einsum('rc,rk->ck', noise, basis, preferred_element_type=jnp.float32)]
    unnamed x9, local copies, waits for them, and re-layouts: 0.9 us -> 0.16 us
    ppermute x3 -> x6, waiting for transfers between devices: 4.91 us -> 4.35 us  [exchange(): lax.ppermute(value, ('rows', 'sub'), [(i, i ^ mask) for i in range(count)])]
  transfers between devices with their start and end apart: 4 -> 6, of which waited for: 3 -> 4; matrix products, arithmetic and copies ran while one was open for 6% -> 11% of each run, Pallas kernels for 0% -> 0%
where the time goes in v1:
time: 20.7 us; the launch traced here: 20.6 us
  starting transfers between devices  10.8 us (52%)
  waiting for transfers between devices  4.35 us (21%)
  matrix products  3.84 us (19%)
  local copies, waits for them, and re-layouts  1.37 us (7%)
    ppermute x6, starting transfers between devices, exchange(): lax.ppermute(value, ('rows', 'sub'), [(i, i ^ mask) for i in range(count)])  10.8 us
    ppermute x6, waiting for transfers between devices, exchange(): lax.ppermute(value, ('rows', 'sub'), [(i, i ^ mask) for i in range(count)])  4.35 us
    dot_general x2, matrix products, per_device(): jnp.einsum('rc,rk->ck', noise, basis, preferred_element_type=jnp.float32)  2.74 us
    add x1, local copies, waits for them, and re-layouts, per_device(): result + jnp.einsum('rk,ck->rc', basis, mapped, preferred_element_type=jn...  1 us
    dot_general x2, matrix products, per_device(): jnp.einsum('rk,ck->rc', basis, mapped, preferred_element_type=jnp.float32)  0.61 us
    dot_general x2, matrix products, per_device(): jnp.dot(other, mixer, precision=lax.Precision.HIGHEST).astype(jnp.bfloat16)  0.48 us
  transfers between devices with their start and end apart: 6, of which 4 were waited for; matrix products, arithmetic and copies ran while one was open for 11% of the time, Pallas kernels for 0%

profile of v1, /device:TPU:0, one launch (start us, length us, event | category | flops | bytes accessed | tf_op | source)
XLA Modules:
  0.0 20.6 jit_solution(11632098686389254188)
XLA Ops:
  0.0 1.4 %convolution_convert_fusion = bf16[128,256]{1,0:T(8,128)(2,1)S(1)} fusion(bf16[1024,128]{1,0:T(8,128)(2,1)} %param.4, bf16[2,1024,256]{2,1,0:T(8,128)(2,1)} %param.5), kind=kOutput, calls=%fused_computation.4 | convolution fusion | flops 67141632 | bytes 851968 | tf_op jit(solution)/shard_map/rc,rk->ck/dot_general | solution.py:35
  1.4 3.1 %collective-permute-start.4 = (bf16[128,256]{1,0:T(8,128)(2,1)S(1)}, bf16[128,256]{1,0:T(8,128)(2,1)S(1)}, u32[]{:S(2)}, u32[]{:S(2)}) collective-permute-start(bf16[128,256]{1,0:T(8,128)(2,1)S(1)} %convolution_convert_fusion), channel_id=1, source_target_pairs={{0,4},{2,6},{4,0},{6,2},{8,12},{10,14},{12,8},{14,10},{1,5},{3,7},... | collective-permute-start | bytes 196616 | tf_op jit(solution)/shard_map/ppermute | solution.py:11
  4.6 1.3 %convolution_convert_fusion.1 = bf16[128,256]{1,0:T(8,128)(2,1)S(1)} fusion(bf16[1024,128]{1,0:T(8,128)(2,1)S(1)} %copy-done.1, bf16[2,1024,256]{2,1,0:T(8,128)(2,1)} %param.5), kind=kOutput, calls=%fused_computation.5 | convolution fusion | flops 67141632 | bytes 851968 | tf_op jit(solution)/shard_map/rc,rk->ck/dot_general | solution.py:35
  5.9 0.0 copy-start.2
  5.9 2.7 %collective-permute-start = (bf16[128,256]{1,0:T(8,128)(2,1)S(1)}, bf16[128,256]{1,0:T(8,128)(2,1)S(1)}, u32[]{:S(2)}, u32[]{:S(2)}) collective-permute-start(bf16[128,256]{1,0:T(8,128)(2,1)S(1)} %convolution_convert_fusion.1), channel_id=1, source_target_pairs={{0,8},{2,10},{4,12},{6,14},{8,0},{10,2},{12,4},{14,6},{1,9},{3,11}... | collective-permute-start | bytes 196616 | tf_op jit(solution)/shard_map/ppermute | solution.py:11
  8.6 0.1 copy.9
  8.8 0.0 collective-permute-done.4
  8.8 1.6 %collective-permute-start.5 = (bf16[128,256]{1,0:T(8,128)(2,1)S(1)}, bf16[128,256]{1,0:T(8,128)(2,1)S(1)}, u32[]{:S(2)}, u32[]{:S(2)}) collective-permute-start(bf16[128,256]{1,0:T(8,128)(2,1)S(1)} %collective-permute-done.4), channel_id=1, source_target_pairs={{0,2},{2,0},{4,6},{6,4},{8,10},{10,8},{12,14},{14,12},{1,3},{3,1},... | collective-permute-start | bytes 196616 | tf_op jit(solution)/shard_map/ppermute | solution.py:11
  10.3 0.1 copy.10
  10.5 0.1 copy.11
  10.6 1.2 %collective-permute-done = bf16[128,256]{1,0:T(8,128)(2,1)S(1)} collective-permute-done((bf16[128,256]{1,0:T(8,128)(2,1)S(1)}, bf16[128,256]{1,0:T(8,128)(2,1)S(1)}, u32[]{:S(2)}, u32[]{:S(2)}) %collective-permute-start) | collective-permute-done | bytes 65568 | tf_op jit(solution)/shard_map/ppermute | solution.py:11
  11.7 0.8 %collective-permute-start.3 = (bf16[128,256]{1,0:T(8,128)(2,1)S(1)}, bf16[128,256]{1,0:T(8,128)(2,1)S(1)}, u32[]{:S(2)}, u32[]{:S(2)}) collective-permute-start(bf16[128,256]{1,0:T(8,128)(2,1)S(1)} %collective-permute-done), channel_id=1, source_target_pairs={{0,6},{2,4},{4,2},{6,0},{8,14},{10,12},{12,10},{14,8},{1,7},{3,5},... | collective-permute-start | bytes 196616 | tf_op jit(solution)/shard_map/ppermute | solution.py:11
  12.5 2.2 %collective-permute-start.2 = (bf16[128,256]{1,0:T(8,128)(2,1)S(1)}, bf16[128,256]{1,0:T(8,128)(2,1)S(1)}, u32[]{:S(2)}, u32[]{:S(2)}) collective-permute-start(bf16[128,256]{1,0:T(8,128)(2,1)S(1)} %collective-permute-done), channel_id=1, source_target_pairs={{0,4},{2,6},{4,0},{6,2},{8,12},{10,14},{12,8},{14,10},{1,5},{3,7},... | collective-permute-start | bytes 196616 | tf_op jit(solution)/shard_map/ppermute | solution.py:11
  14.7 0.5 %collective-permute-start.1 = (bf16[128,256]{1,0:T(8,128)(2,1)S(1)}, bf16[128,256]{1,0:T(8,128)(2,1)S(1)}, u32[]{:S(2)}, u32[]{:S(2)}) collective-permute-start(bf16[128,256]{1,0:T(8,128)(2,1)S(1)} %collective-permute-done), channel_id=1, source_target_pairs={{0,2},{2,0},{4,6},{6,4},{8,10},{10,8},{12,14},{14,12},{1,3},{3,1},... | collective-permute-start | bytes 196616 | tf_op jit(solution)/shard_map/ppermute | solution.py:11
  15.2 0.0 collective-permute-done.5
  15.2 0.2 %convolution_convert_fusion.2 = bf16[128,256]{1,0:T(8,128)(2,1)S(1)} fusion(bf16[256,256]{1,0:T(8,128)(2,1)S(1)} %get-tuple-element.6, bf16[256,256]{0,1:T(8,128)(2,1)S(1)} %copy.11, bf16[128,256]{1,0:T(8,128)(2,1)S(1)} %collective-permute-done.5, bf16[128,256]{1,0:T(8,128)(2,1)S(1)} %collective-permute-done.4, pred[]{:T(512)S(6)} %eq.10), kind=kOutput, calls=%fused_computation.6 | convolution fusion | flops 100859904 | bytes 458753 | tf_op jit(solution)/shard_map/dot_general | solution.py:43
  15.5 0.3 %convolution_bitcast_fusion = f32[1024,128]{0,1:T(8,128)S(1)} fusion(bf16[128,256]{1,0:T(8,128)(2,1)S(1)} %convolution_convert_fusion.2, bf16[2,1024,256]{2,1,0:T(8,128)(2,1)S(1)} %copy-done), kind=kOutput, calls=%fused_computation | convolution fusion | flops 67108864 | bytes 1114112 | tf_op jit(solution)/shard_map/rk,ck->rc/dot_general | solution.py:44
  15.8 0.0 copy-start.3
  15.8 1.3 %collective-permute-done.3 = bf16[128,256]{1,0:T(8,128)(2,1)S(1)} collective-permute-done((bf16[128,256]{1,0:T(8,128)(2,1)S(1)}, bf16[128,256]{1,0:T(8,128)(2,1)S(1)}, u32[]{:S(2)}, u32[]{:S(2)}) %collective-permute-start.3) | collective-permute-done | bytes 65568 | tf_op jit(solution)/shard_map/ppermute | solution.py:11
  17.1 0.6 %collective-permute-done.2 = bf16[128,256]{1,0:T(8,128)(2,1)S(1)} collective-permute-done((bf16[128,256]{1,0:T(8,128)(2,1)S(1)}, bf16[128,256]{1,0:T(8,128)(2,1)S(1)}, u32[]{:S(2)}, u32[]{:S(2)}) %collective-permute-start.2) | collective-permute-done | bytes 65568 | tf_op jit(solution)/shard_map/ppermute | solution.py:11
  17.7 1.3 %collective-permute-done.1 = bf16[128,256]{1,0:T(8,128)(2,1)S(1)} collective-permute-done((bf16[128,256]{1,0:T(8,128)(2,1)S(1)}, bf16[128,256]{1,0:T(8,128)(2,1)S(1)}, u32[]{:S(2)}, u32[]{:S(2)}) %collective-permute-start.1) | collective-permute-done | bytes 65568 | tf_op jit(solution)/shard_map/ppermute | solution.py:11
  19.0 0.2 %convolution_convert_fusion.3 = bf16[128,256]{1,0:T(8,128)(2,1)S(1)} fusion(bf16[256,256]{1,0:T(8,128)(2,1)S(1)} %get-tuple-element.5, bf16[256,256]{0,1:T(8,128)(2,1)S(1)} %copy.10, bf16[128,256]{1,0:T(8,128)(2,1)S(1)} %collective-permute-done.3, bf16[128,256]{1,0:T(8,128)(2,1)S(1)} %collective-permute-done.2, ...), kind=kOutput, calls=%fused_computation.7 | convolution fusion | flops 100990976 | bytes 589825 | tf_op jit(solution)/shard_map/dot_general | solution.py:43
  19.2 0.3 %fusion.1 = f32[1024,128]{0,1:T(8,128)S(1)} fusion(f32[1024,128]{0,1:T(8,128)S(1)} %convolution_bitcast_fusion, bf16[128,256]{1,0:T(8,128)(2,1)S(1)} %convolution_convert_fusion.3, bf16[1024,128]{0,1:T(8,128)(2,1)S(1)} %copy.9, bf16[2,1024,256]{2,1,0:T(8,128)(2,1)S(1)} %copy-done, f32[1024]{0:T(1024)S(1)} %copy-done.3), kind=kOutput, calls=%fused_computation.3 | convolution fusion | flops 67633152 | bytes 1904640 | tf_op jit(solution)/shard_map/rk,ck->rc/dot_general | solution.py:44
  19.6 1.0 %copy.12 = f32[1024,128]{1,0:T(8,128)} copy(f32[1024,128]{0,1:T(8,128)S(1)} %fusion.1) | data formatting | bytes 1048576 | tf_op jit(solution)/shard_map/add | solution.py:44
  (7 shorter events, 0.0 us)
Async XLA Ops:
  0.0 4.6 %copy-start.1 = (bf16[1024,128]{1,0:T(8,128)(2,1)S(1)}, bf16[1024,128]{1,0:T(8,128)(2,1)}, u32[]{:S(2)}) copy-start(bf16[1024,128]{1,0:T(8,128)(2,1)} %param.4) | copy-start | bytes 786436
  1.4 7.3 %collective-permute-start.4 = (bf16[128,256]{1,0:T(8,128)(2,1)S(1)}, bf16[128,256]{1,0:T(8,128)(2,1)S(1)}, u32[]{:S(2)}, u32[]{:S(2)}) collective-permute-start(bf16[128,256]{1,0:T(8,128)(2,1)S(1)} %convolution_convert_fusion), channel_id=1, source_target_pairs={{0,4},{2,6},{4,0},{6,2},{8,12},{10,14},{12,8},{14,10},{1,5},{3,7},... | collective-permute-start | bytes 196616 | tf_op jit(solution)/shard_map/ppermute | solution.py:11
  5.9 4.4 %copy-start.2 = (bf16[3,256,256]{2,1,0:T(8,128)(2,1)S(1)}, bf16[3,256,256]{2,1,0:T(8,128)(2,1)}, u32[]{:S(2)}) copy-start(bf16[3,256,256]{2,1,0:T(8,128)(2,1)} %param.6) | copy-start | bytes 1179652
  5.9 5.8 %collective-permute-start = (bf16[128,256]{1,0:T(8,128)(2,1)S(1)}, bf16[128,256]{1,0:T(8,128)(2,1)S(1)}, u32[]{:S(2)}, u32[]{:S(2)}) collective-permute-start(bf16[128,256]{1,0:T(8,128)(2,1)S(1)} %convolution_convert_fusion.1), channel_id=1, source_target_pairs={{0,8},{2,10},{4,12},{6,14},{8,0},{10,2},{12,4},{14,6},{1,9},{3,11}... | collective-permute-start | bytes 196616 | tf_op jit(solution)/shard_map/ppermute | solution.py:11
  8.5 6.9 %copy-start = (bf16[2,1024,256]{2,1,0:T(8,128)(2,1)S(1)}, bf16[2,1024,256]{2,1,0:T(8,128)(2,1)}, u32[]{:S(2)}) copy-start(bf16[2,1024,256]{2,1,0:T(8,128)(2,1)} %param.5) | copy-start | bytes 3145732
  8.8 6.5 %collective-permute-start.5 = (bf16[128,256]{1,0:T(8,128)(2,1)S(1)}, bf16[128,256]{1,0:T(8,128)(2,1)S(1)}, u32[]{:S(2)}, u32[]{:S(2)}) collective-permute-start(bf16[128,256]{1,0:T(8,128)(2,1)S(1)} %collective-permute-done.4), channel_id=1, source_target_pairs={{0,2},{2,0},{4,6},{6,4},{8,10},{10,8},{12,14},{14,12},{1,3},{3,1},... | collective-permute-start | bytes 196616 | tf_op jit(solution)/shard_map/ppermute | solution.py:11
  11.7 5.4 %collective-permute-start.3 = (bf16[128,256]{1,0:T(8,128)(2,1)S(1)}, bf16[128,256]{1,0:T(8,128)(2,1)S(1)}, u32[]{:S(2)}, u32[]{:S(2)}) collective-permute-start(bf16[128,256]{1,0:T(8,128)(2,1)S(1)} %collective-permute-done), channel_id=1, source_target_pairs={{0,6},{2,4},{4,2},{6,0},{8,14},{10,12},{12,10},{14,8},{1,7},{3,5},... | collective-permute-start | bytes 196616 | tf_op jit(solution)/shard_map/ppermute | solution.py:11
  12.5 5.2 %collective-permute-start.2 = (bf16[128,256]{1,0:T(8,128)(2,1)S(1)}, bf16[128,256]{1,0:T(8,128)(2,1)S(1)}, u32[]{:S(2)}, u32[]{:S(2)}) collective-permute-start(bf16[128,256]{1,0:T(8,128)(2,1)S(1)} %collective-permute-done), channel_id=1, source_target_pairs={{0,4},{2,6},{4,0},{6,2},{8,12},{10,14},{12,8},{14,10},{1,5},{3,7},... | collective-permute-start | bytes 196616 | tf_op jit(solution)/shard_map/ppermute | solution.py:11
  14.7 4.3 %collective-permute-start.1 = (bf16[128,256]{1,0:T(8,128)(2,1)S(1)}, bf16[128,256]{1,0:T(8,128)(2,1)S(1)}, u32[]{:S(2)}, u32[]{:S(2)}) collective-permute-start(bf16[128,256]{1,0:T(8,128)(2,1)S(1)} %collective-permute-done), channel_id=1, source_target_pairs={{0,2},{2,0},{4,6},{6,4},{8,10},{10,8},{12,14},{14,12},{1,3},{3,1},... | collective-permute-start | bytes 196616 | tf_op jit(solution)/shard_map/ppermute | solution.py:11
  15.8 3.4 %copy-start.3 = (f32[1024]{0:T(1024)S(1)}, f32[1024]{0:T(1024)}, u32[]{:S(2)}) copy-start(f32[1024]{0:T(1024)} %param.7) | copy-start | bytes 12292

commit v2 on v1

v2 whole, which is shorter than its diff:
```python
import functools

import jax
import jax.numpy as jnp
from jax import lax
from jax.experimental import pallas as pl
from jax.experimental.pallas import tpu as pltpu
from jax.sharding import PartitionSpec as P

VMEM = pl.BlockSpec(memory_space=pltpu.VMEM)
HBM = pl.BlockSpec(memory_space=pltpu.HBM)
ANY = pl.BlockSpec(memory_space=pl.ANY)
PARAMS = pltpu.CompilerParams(vmem_limit_bytes=8 * 2**20)
CHUNKS = 4


def f32(value):
    return value.astype(jnp.float32)


def cost(flops, bytes_accessed):
    return pl.CostEstimate(flops=flops, bytes_accessed=bytes_accessed, transcendentals=0)


def exchange(value, row_mask, sub_mask, col_mask):
    subs, cols = lax.axis_size("sub"), lax.axis_size("cols")
    count = lax.axis_size("rows") * subs * cols
    mask = (row_mask * subs + sub_mask) * cols + col_mask
    return lax.ppermute(value, ("rows", "sub", "cols"), [(i, i ^ mask) for i in range(count)])


def project_onto(noise, basis):
    return lax.dot_general(
        noise, basis, (((0,), (0,)), ((), ())), preferred_element_type=jnp.float32
    ).astype(jnp.bfloat16)


def load_kernel(noise_hbm, bases_hbm, noise_ref, bases_ref, out_ref, sems):
    count = bases_ref.shape[0]
    copies = [pltpu.make_async_copy(noise_hbm, noise_ref, sems.at[count])]
    copies += [
        pltpu.make_async_copy(bases_hbm.at[level], bases_ref.at[level], sems.at[level])
        for level in range(count)
    ]
    for copy in copies:
        copy.start()
    copies[0].wait()
    copies[1].wait()
    out_ref[...] = project_onto(noise_ref[...], bases_ref[0])
    for copy in copies[2:]:
        copy.wait()


def load(noise, bases):
    size, cols = noise.shape
    count, _, rank = bases.shape
    return pl.pallas_call(
        load_kernel,
        out_shape=(
            jax.ShapeDtypeStruct(noise.shape, noise.dtype),
            jax.ShapeDtypeStruct(bases.shape, bases.dtype),
            jax.ShapeDtypeStruct((cols, rank), jnp.bfloat16),
        ),
        in_specs=[HBM, HBM],
        out_specs=(VMEM, VMEM, VMEM),
        scratch_shapes=[pltpu.SemaphoreType.DMA((count + 1,))],
        compiler_params=PARAMS,
        cost_estimate=cost(2 * size * cols * rank, 2 * size * (cols + count * rank)),
    )(
        pltpu.with_memory_space_constraint(noise, pltpu.HBM),
        pltpu.with_memory_space_constraint(bases, pltpu.HBM),
    )


def project_kernel(level, noise_ref, bases_ref, out_ref):
    out_ref[...] = project_onto(noise_ref[...], bases_ref[level])


def project(noise, bases, level):
    size, cols = noise.shape
    rank = bases.shape[2]
    return pl.pallas_call(
        functools.partial(project_kernel, level),
        out_shape=jax.ShapeDtypeStruct((cols, rank), jnp.bfloat16),
        in_specs=[VMEM, VMEM],
        out_specs=VMEM,
        compiler_params=PARAMS,
        cost_estimate=cost(2 * size * cols * rank, 2 * size * (cols + rank)),
    )(noise, bases)


def mixer_kernel(depth, cores_ref, out_ref):
    place = lax.axis_index("rows")
    for level in range(out_ref.shape[0]):
        node = place // 2 ** (depth - level - 1)
        core = cores_ref[2**level - 1 + node // 2]

        @pl.when(node % 2 == 1)
        def _():
            out_ref[level] = core

        @pl.when(node % 2 == 0)
        def _():
            out_ref[level] = core.T


def halves(value):
    high = value.astype(jnp.bfloat16)
    return jnp.concatenate([high, (value - f32(high)).astype(jnp.bfloat16)], axis=0)


def mapped(mixer, part_refs):
    total = f32(part_refs[0][...])
    for ref in part_refs[1:]:
        total = total + f32(ref[...])
    both = jnp.dot(halves(total), mixer, preferred_element_type=jnp.float32)
    cols = total.shape[0]
    return halves(both[:cols] + both[cols:])


def spread(basis, weights):
    both = lax.dot_general(
        basis, weights, (((1,), (1,)), ((), ())), preferred_element_type=jnp.float32
    )
    cols = weights.shape[0] // 2
    return both[:, :cols] + both[:, cols:]


def first_kernel(level, noise_ref, mob_ref, bases_ref, mixer_ref, *refs):
    part_refs, out_ref = refs[:-1], refs[-1]
    weights = mapped(mixer_ref[level], part_refs)
    mob = mob_ref[...].T
    rows = mob.shape[0]
    for i in range(mob.shape[1]):
        part = pl.ds(i * rows, rows)
        out_ref[part, :] = mob[:, i : i + 1] * f32(noise_ref[part, :]) + spread(
            bases_ref[level, part, :], weights
        )


def next_kernel(level, sum_ref, bases_ref, mixer_ref, *refs):
    part_refs, out_ref = refs[:-1], refs[-1]
    out_ref[...] = sum_ref[...] + spread(bases_ref[level], mapped(mixer_ref[level], part_refs))


def last_kernel(level, sum_ref, bases_ref, mixer_ref, *refs):
    part_refs, out_hbm, buf, sems = refs[:-3], refs[-3], refs[-2], refs[-1]
    weights = mapped(mixer_ref[level], part_refs)
    rows = buf.shape[0] // CHUNKS
    copies = []
    for i in range(CHUNKS):
        part = pl.ds(i * rows, rows)
        buf[part, :] = sum_ref[part, :] + spread(bases_ref[level, part, :], weights)
        copies.append(pltpu.make_async_copy(buf.at[part], out_hbm.at[part], sems.at[i]))
        copies[-1].start()
    for copy in copies:
        copy.wait()


def gather(level, proj, depth, sub_bits):
    swap = 2 ** (depth - level - 1)
    bits = [(0, 2**b) for b in range(sub_bits)] + [(2**b, 0) for b in range(depth - level - 1)]
    if level > 0 and len(bits) < 2:
        return [
            exchange(proj, swap ^ row_mask, sub_mask, 0)
            for row_mask, sub_mask in [(0, 0)] + bits
        ]
    flip = lax.axis_size("cols") - 1
    value = exchange(proj, swap, 0, flip)
    if not bits:
        return [exchange(value, 0, 0, flip) if flip else value]
    while bits:
        now, bits = bits[:2], bits[2:]
        masks = list(now)
        if len(now) == 2:
            masks.append((now[0][0] ^ now[1][0], now[0][1] ^ now[1][1]))
        terms = [exchange(value, *mask, flip) for mask in masks]
        terms.append(exchange(value, 0, 0, flip) if flip else value)
        if bits:
            value, flip = sum(f32(term) for term in terms), 0
    return terms


def per_device(noise, bases, cores, self_mob):
    depth = lax.axis_size("rows").bit_length() - 1
    sub_bits = lax.axis_size("sub").bit_length() - 1
    size, cols = noise.shape
    count, _, rank = bases.shape
    lanes = 128
    noise, bases, first = load(noise, bases)
    parts = []
    for level in range(count):
        proj = project(noise, bases, level) if level else first
        parts.append(gather(level, proj, depth, sub_bits))
    mixer = pl.pallas_call(
        functools.partial(mixer_kernel, depth),
        out_shape=jax.ShapeDtypeStruct((count, *cores.shape[1:]), cores.dtype),
        in_specs=[VMEM],
        out_specs=VMEM,
        compiler_params=PARAMS,
        cost_estimate=cost(0, cores.size * 4),
    )(cores)
    shape = jax.ShapeDtypeStruct((size, cols), jnp.float32)
    estimate = cost(4 * size * cols * rank, size * cols * 8)
    result = None
    for level in range(count - 1, 0, -1):
        if result is None:
            kernel, operands = first_kernel, (noise, self_mob.reshape(size // lanes, lanes))
        else:
            kernel, operands = next_kernel, (result,)
        operands += (bases, mixer, *parts[level])
        result = pl.pallas_call(
            functools.partial(kernel, level),
            out_shape=shape,
            in_specs=[VMEM] * len(operands),
            out_specs=VMEM,
            compiler_params=PARAMS,
            cost_estimate=estimate,
        )(*operands)
    if result is None:
        result = self_mob[:, None] * f32(noise)
    operands = (result, bases, mixer, *parts[0])
    return pl.pallas_call(
        functools.partial(last_kernel, 0),
        out_shape=shape,
        in_specs=[VMEM] * len(operands),
        out_specs=ANY,
        scratch_shapes=[pltpu.VMEM((size, cols), jnp.float32), pltpu.SemaphoreType.DMA((CHUNKS,))],
        compiler_params=PARAMS,
        cost_estimate=estimate,
    )(*operands)


def solution(mesh):
    in_specs = (
        P(("groups", "rows", "sub"), "cols"),
        P(None, ("groups", "rows", "sub"), None),
        P("groups", None, None),
        P(("groups", "rows", "sub")),
    )
    out_specs = P(("groups", "rows", "sub"), "cols")
    return jax.shard_map(
        per_device, mesh=mesh, in_specs=in_specs, out_specs=out_specs, check_vma=False
    )
```

time: 20.7 us -> 17.7 us (0.86)
  Pallas kernels: 0 us -> 3.87 us
  matrix products: 3.84 us -> 0 us
  waiting for transfers between devices: 4.35 us -> 2.61 us
  local copies, waits for them, and re-layouts: 1.37 us -> 0.46 us
    pallas_call x0 -> x5, Pallas kernels: none -> 3.87 us  [the longest x1 1.43 us: load(): pl.pallas_call(load_kernel, out_shape=(jax.ShapeDtypeStruct(noise.shape,...]
    dot_general x6 -> x0, matrix products: 3.84 us -> none  [the longest x2 2.74 us: per_device(): jnp.einsum('rc,rk->ck', noise, basis, preferred_element_type=jnp.float32)]
    ppermute x6 -> x7, waiting for transfers between devices: 4.35 us -> 2.61 us  [exchange(): lax.ppermute(value, ('rows', 'sub', 'cols'), [(i, i ^ mask) for i in rang...]
    add x1 -> x0, local copies, waits for them, and re-layouts: 1 us -> none  [per_device(): result + jnp.einsum('rk,ck->rc', basis, mapped, preferred_element_type=jn...]
    unnamed x9 -> x4, local copies, waits for them, and re-layouts: 0.16 us -> 0.46 us
    ppermute x6 -> x7, starting transfers between devices: 10.8 us -> 10.6 us  [exchange(): lax.ppermute(value, ('rows', 'sub', 'cols'), [(i, i ^ mask) for i in rang...]
    squeeze x3 -> x0, local copies, waits for them, and re-layouts: 0.22 us -> none  [per_device(): lax.dynamic_index_in_dim(cores, 2 ** (level - 1) - 1 + node // 2, 0, keep...]
  transfers between devices with their start and end apart: 6 -> 7, of which waited for: 4 -> 3; matrix products, arithmetic and copies ran while one was open for 11% -> 0% of each run, Pallas kernels for 0% -> 7%
where the time goes in v2:
time: 17.7 us; the launch traced here: 17.6 us
  starting transfers between devices  10.6 us (60%)
  Pallas kernels  3.87 us (22%)
  waiting for transfers between devices  2.61 us (15%)
  local copies, waits for them, and re-layouts  0.46 us (3%)
    ppermute x7, starting transfers between devices, exchange(): lax.ppermute(value, ('rows', 'sub', 'cols'), [(i, i ^ mask) for i in rang...  10.6 us
    ppermute x7, waiting for transfers between devices, exchange(): lax.ppermute(value, ('rows', 'sub', 'cols'), [(i, i ^ mask) for i in rang...  2.61 us
    pallas_call x1, Pallas kernels, load(): pl.pallas_call(load_kernel, out_shape=(jax.ShapeDtypeStruct(noise.shape,...  1.43 us
    pallas_call x1, Pallas kernels, per_device(): pl.pallas_call(functools.partial(last_kernel, 0), out_shape=shape, in_spe...  1.27 us
    pallas_call x1, Pallas kernels, per_device(): pl.pallas_call(functools.partial(kernel, level), out_shape=shape, in_spec...  0.7 us
    unnamed x4, local copies, waits for them, and re-layouts  0.46 us
  transfers between devices with their start and end apart: 7, of which 3 were waited for; matrix products, arithmetic and copies ran while one was open for 0% of the time, Pallas kernels for 7%

profile of v2, /device:TPU:0, one launch (start us, length us, event | category | flops | bytes accessed | tf_op | source)
XLA Modules:
  0.0 17.6 jit_solution(5804420741214673082)
XLA Ops:
  0.0 1.4 %shard_map.46 = (bf16[1024,128]{1,0:T(8,128)(2,1)S(1)}, bf16[2,1024,256]{2,1,0:T(8,128)(2,1)S(1)}, bf16[128,256]{1,0:T(8,128)(2,1)S(1)}) custom-call(bf16[1024,128]{1,0:T(8,128)(2,1)} %noise_hbm.1, bf16[2,1024,256]{2,1,0:T(8,128)(2,1)} %bases_hbm.1), custom_call_target="tpu_custom_call" | custom-call | flops 67108864 | bytes 1310720 | tf_op jit(solution)/shard_map/pallas_call | solution.py:57
  1.4 3.6 %collective-permute-start.2 = (bf16[128,256]{1,0:T(8,128)(2,1)S(1)}, bf16[128,256]{1,0:T(8,128)(2,1)S(1)}, u32[]{:S(2)}, u32[]{:S(2)}) collective-permute-start(bf16[128,256]{1,0:T(8,128)(2,1)S(1)} %get-tuple-element.10), channel_id=1, source_target_pairs={{0,9},{1,8},{2,11},{3,10},{4,13},{5,12},{6,15},{7,14},{8,1},{9,0},... | collective-permute-start | bytes 196616 | tf_op jit(solution)/shard_map/ppermute | solution.py:29
  5.0 0.0 copy-start
  5.0 0.3 %shard_map.48 = bf16[128,256]{1,0:T(8,128)(2,1)S(1)} custom-call(bf16[1024,128]{1,0:T(8,128)(2,1)S(1)} %get-tuple-element.8.noise_ref, bf16[2,1024,256]{2,1,0:T(8,128)(2,1)S(1)} %get-tuple-element.9.bases_ref), custom_call_target="tpu_custom_call" | custom-call | flops 67108864 | bytes 786432 | tf_op jit(solution)/shard_map/pallas_call | solution.py:82
  5.3 2.6 %collective-permute-start.1 = (bf16[128,256]{1,0:T(8,128)(2,1)S(1)}, bf16[128,256]{1,0:T(8,128)(2,1)S(1)}, u32[]{:S(2)}, u32[]{:S(2)}) collective-permute-start(bf16[128,256]{1,0:T(8,128)(2,1)S(1)} %shard_map.48), channel_id=1, source_target_pairs={{0,6},{1,7},{2,4},{3,5},{4,2},{5,3},{6,0},{7,1},{8,14},{9,15},{10,... | collective-permute-start | bytes 196616 | tf_op jit(solution)/shard_map/ppermute | solution.py:29
  7.9 0.5 %collective-permute-start = (bf16[128,256]{1,0:T(8,128)(2,1)S(1)}, bf16[128,256]{1,0:T(8,128)(2,1)S(1)}, u32[]{:S(2)}, u32[]{:S(2)}) collective-permute-start(bf16[128,256]{1,0:T(8,128)(2,1)S(1)} %shard_map.48), channel_id=1, source_target_pairs={{0,4},{1,5},{2,6},{3,7},{4,0},{5,1},{6,2},{7,3},{8,12},{9,13},{10,... | collective-permute-start | bytes 196616 | tf_op jit(solution)/shard_map/ppermute | solution.py:29
  8.3 0.0 collective-permute-done.2
  8.3 0.1 collective-permute-start.6
  8.4 3.0 %collective-permute-start.5 = (bf16[128,256]{1,0:T(8,128)(2,1)S(1)}, bf16[128,256]{1,0:T(8,128)(2,1)S(1)}, u32[]{:S(2)}, u32[]{:S(2)}) collective-permute-start(bf16[128,256]{1,0:T(8,128)(2,1)S(1)} %collective-permute-done.2), channel_id=1, source_target_pairs={{0,7},{1,6},{2,5},{3,4},{4,3},{5,2},{6,1},{7,0},{8,15},{9,14},{10,... | collective-permute-start | bytes 196616 | tf_op jit(solution)/shard_map/ppermute | solution.py:29
  11.4 0.8 %collective-permute-start.4 = (bf16[128,256]{1,0:T(8,128)(2,1)S(1)}, bf16[128,256]{1,0:T(8,128)(2,1)S(1)}, u32[]{:S(2)}, u32[]{:S(2)}) collective-permute-start(bf16[128,256]{1,0:T(8,128)(2,1)S(1)} %collective-permute-done.2), channel_id=1, source_target_pairs={{0,5},{1,4},{2,7},{3,6},{4,1},{5,0},{6,3},{7,2},{8,13},{9,12},{10,... | collective-permute-start | bytes 196616 | tf_op jit(solution)/shard_map/ppermute | solution.py:29
  12.3 0.0 collective-permute-done.1.refs_1_
  12.3 0.0 collective-permute-start.3
  12.3 0.0 copy-done
  12.3 0.0 copy-start.1
  12.3 0.2 %shard_map.47.mixer_ref = bf16[2,256,256]{2,1,0:T(8,128)(2,1)S(1)} custom-call(bf16[3,256,256]{2,1,0:T(8,128)(2,1)S(1)} %copy-done), custom_call_target="tpu_custom_call" | custom-call | bytes 786432 | tf_op jit(solution)/shard_map/pallas_call | solution.py:195
  12.5 0.0 collective-permute-done.refs_0_
  12.5 0.5 %copy-done.1 = f32[1024]{0:T(1024)S(1)} copy-done((f32[1024]{0:T(1024)S(1)}, f32[1024]{0:T(1024)}, u32[]{:S(2)}) %copy-start.1) | copy-done | bytes 4120
  13.0 0.7 %shard_map.49.sum_ref = f32[1024,128]{1,0:T(8,128)S(1)} custom-call(bf16[1024,128]{1,0:T(8,128)(2,1)S(1)} %get-tuple-element.8.noise_ref, f32[8,128]{1,0:T(8,128)S(1)} %bitcast.1, bf16[2,1024,256]{2,1,0:T(8,128)(2,1)S(1)} %get-tuple-element.9.bases_ref, bf16[2,256,256]{2,1,0:T(8,128)(2,1)S(1)} %shard_map.47.mixer_ref, ...), custom_call_target="tpu_custom_call" | custom-call | flops 134217728 | bytes 1048576 | tf_op jit(solution)/shard_map/pallas_call | solution.py:212
  13.7 0.0 collective-permute-done.6.refs_3_
  13.7 0.2 collective-permute-done.5.refs_2_
  13.8 2.1 %collective-permute-done.4.refs_1_ = bf16[128,256]{1,0:T(8,128)(2,1)S(1)} collective-permute-done((bf16[128,256]{1,0:T(8,128)(2,1)S(1)}, bf16[128,256]{1,0:T(8,128)(2,1)S(1)}, u32[]{:S(2)}, u32[]{:S(2)}) %collective-permute-start.4) | collective-permute-done | bytes 65568 | tf_op jit(solution)/shard_map/ppermute | solution.py:29
  15.9 0.3 %collective-permute-done.3.refs_0_ = bf16[128,256]{1,0:T(8,128)(2,1)S(1)} collective-permute-done((bf16[128,256]{1,0:T(8,128)(2,1)S(1)}, bf16[128,256]{1,0:T(8,128)(2,1)S(1)}, u32[]{:S(2)}, u32[]{:S(2)}) %collective-permute-start.3) | collective-permute-done | bytes 65568 | tf_op jit(solution)/shard_map/ppermute | solution.py:29
  16.3 1.3 %shard_map.50 = f32[1024,128]{1,0:T(8,128)} custom-call(f32[1024,128]{1,0:T(8,128)S(1)} %shard_map.49.sum_ref, bf16[2,1024,256]{2,1,0:T(8,128)(2,1)S(1)} %get-tuple-element.9.bases_ref, bf16[2,256,256]{2,1,0:T(8,128)(2,1)S(1)} %shard_map.47.mixer_ref, bf16[128,256]{1,0:T(8,128)(2,1)S(1)} %collective-permute-done.3.refs_0_, ...), custom_call_target="tpu_custom_call" | custom-call | flops 134217728 | bytes 1048576 | tf_op jit(solution)/shard_map/pallas_call | solution.py:223
Async XLA Ops:
  1.4 6.9 %collective-permute-start.2 = (bf16[128,256]{1,0:T(8,128)(2,1)S(1)}, bf16[128,256]{1,0:T(8,128)(2,1)S(1)}, u32[]{:S(2)}, u32[]{:S(2)}) collective-permute-start(bf16[128,256]{1,0:T(8,128)(2,1)S(1)} %get-tuple-element.10), channel_id=1, source_target_pairs={{0,9},{1,8},{2,11},{3,10},{4,13},{5,12},{6,15},{7,14},{8,1},{9,0},... | collective-permute-start | bytes 196616 | tf_op jit(solution)/shard_map/ppermute | solution.py:29
  5.0 7.3 %copy-start = (bf16[3,256,256]{2,1,0:T(8,128)(2,1)S(1)}, bf16[3,256,256]{2,1,0:T(8,128)(2,1)}, u32[]{:S(2)}) copy-start(bf16[3,256,256]{2,1,0:T(8,128)(2,1)} %cores_ref.1) | copy-start | bytes 1179652
  5.3 7.0 %collective-permute-start.1 = (bf16[128,256]{1,0:T(8,128)(2,1)S(1)}, bf16[128,256]{1,0:T(8,128)(2,1)S(1)}, u32[]{:S(2)}, u32[]{:S(2)}) collective-permute-start(bf16[128,256]{1,0:T(8,128)(2,1)S(1)} %shard_map.48), channel_id=1, source_target_pairs={{0,6},{1,7},{2,4},{3,5},{4,2},{5,3},{6,0},{7,1},{8,14},{9,15},{10,... | collective-permute-start | bytes 196616 | tf_op jit(solution)/shard_map/ppermute | solution.py:29
  7.9 4.7 %collective-permute-start = (bf16[128,256]{1,0:T(8,128)(2,1)S(1)}, bf16[128,256]{1,0:T(8,128)(2,1)S(1)}, u32[]{:S(2)}, u32[]{:S(2)}) collective-permute-start(bf16[128,256]{1,0:T(8,128)(2,1)S(1)} %shard_map.48), channel_id=1, source_target_pairs={{0,4},{1,5},{2,6},{3,7},{4,0},{5,1},{6,2},{7,3},{8,12},{9,13},{10,... | collective-permute-start | bytes 196616 | tf_op jit(solution)/shard_map/ppermute | solution.py:29
  8.3 5.4 %collective-permute-start.6 = (bf16[128,256]{1,0:T(8,128)(2,1)S(1)}, bf16[128,256]{1,0:T(8,128)(2,1)S(1)}, u32[]{:S(2)}, u32[]{:S(2)}) collective-permute-start(bf16[128,256]{1,0:T(8,128)(2,1)S(1)} %collective-permute-done.2), channel_id=1, source_target_pairs={{0,1},{1,0},{2,3},{3,2},{4,5},{5,4},{6,7},{7,6},{8,9},{9,8},{10,11... | collective-permute-start | bytes 196616 | tf_op jit(solution)/shard_map/ppermute | solution.py:29
  8.4 5.4 %collective-permute-start.5 = (bf16[128,256]{1,0:T(8,128)(2,1)S(1)}, bf16[128,256]{1,0:T(8,128)(2,1)S(1)}, u32[]{:S(2)}, u32[]{:S(2)}) collective-permute-start(bf16[128,256]{1,0:T(8,128)(2,1)S(1)} %collective-permute-done.2), channel_id=1, source_target_pairs={{0,7},{1,6},{2,5},{3,4},{4,3},{5,2},{6,1},{7,0},{8,15},{9,14},{10,... | collective-permute-start | bytes 196616 | tf_op jit(solution)/shard_map/ppermute | solution.py:29
  11.4 4.5 %collective-permute-start.4 = (bf16[128,256]{1,0:T(8,128)(2,1)S(1)}, bf16[128,256]{1,0:T(8,128)(2,1)S(1)}, u32[]{:S(2)}, u32[]{:S(2)}) collective-permute-start(bf16[128,256]{1,0:T(8,128)(2,1)S(1)} %collective-permute-done.2), channel_id=1, source_target_pairs={{0,5},{1,4},{2,7},{3,6},{4,1},{5,0},{6,3},{7,2},{8,13},{9,12},{10,... | collective-permute-start | bytes 196616 | tf_op jit(solution)/shard_map/ppermute | solution.py:29
  12.3 4.0 %collective-permute-start.3 = (bf16[128,256]{1,0:T(8,128)(2,1)S(1)}, bf16[128,256]{1,0:T(8,128)(2,1)S(1)}, u32[]{:S(2)}, u32[]{:S(2)}) collective-permute-start(bf16[128,256]{1,0:T(8,128)(2,1)S(1)} %collective-permute-done.2), channel_id=1, source_target_pairs={{0,3},{1,2},{2,1},{3,0},{4,7},{5,6},{6,5},{7,4},{8,11},{9,10},{10,... | collective-permute-start | bytes 196616 | tf_op jit(solution)/shard_map/ppermute | solution.py:29
  12.3 0.7 %copy-start.1 = (f32[1024]{0:T(1024)S(1)}, f32[1024]{0:T(1024)}, u32[]{:S(2)}) copy-start(f32[1024]{0:T(1024)} %param.7) | copy-start | bytes 12292

commit v3 on v2

--- a/solution.py
+++ b/solution.py
@@ -32,10 +32,10 @@
 def project_onto(noise, basis):
     return lax.dot_general(
         noise, basis, (((0,), (0,)), ((), ())), preferred_element_type=jnp.float32
-    ).astype(jnp.bfloat16)
-
-
-def load_kernel(noise_hbm, bases_hbm, noise_ref, bases_ref, out_ref, sems):
+    )
+
+
+def load_kernel(noise_hbm, bases_hbm, noise_ref, bases_ref, out_ref, wide_ref, sems):
     count = bases_ref.shape[0]
     copies = [pltpu.make_async_copy(noise_hbm, noise_ref, sems.at[count])]
     copies += [
@@ -46,7 +46,9 @@
         copy.start()
     copies[0].wait()
     copies[1].wait()
-    out_ref[...] = project_onto(noise_ref[...], bases_ref[0])
+    proj = project_onto(noise_ref[...], bases_ref[0])
+    out_ref[...] = proj.astype(out_ref.dtype)
+    wide_ref[...] = proj
     for copy in copies[2:]:
         copy.wait()
 
@@ -60,9 +62,10 @@
             jax.ShapeDtypeStruct(noise.shape, noise.dtype),
             jax.ShapeDtypeStruct(bases.shape, bases.dtype),
             jax.ShapeDtypeStruct((cols, rank), jnp.bfloat16),
+            jax.ShapeDtypeStruct((cols, rank), jnp.float32),
         ),
         in_specs=[HBM, HBM],
-        out_specs=(VMEM, VMEM, VMEM),
+        out_specs=(VMEM, VMEM, VMEM, VMEM),
         scratch_shapes=[pltpu.SemaphoreType.DMA((count + 1,))],
         compiler_params=PARAMS,
         cost_estimate=cost(2 * size * cols * rank, 2 * size * (cols + count * rank)),
@@ -73,7 +76,7 @@
 
 
 def project_kernel(level, noise_ref, bases_ref, out_ref):
-    out_ref[...] = project_onto(noise_ref[...], bases_ref[level])
+    out_ref[...] = project_onto(noise_ref[...], bases_ref[level]).astype(out_ref.dtype)
 
 
 def project(noise, bases, level):
@@ -157,7 +160,7 @@
         copy.wait()
 
 
-def gather(level, proj, depth, sub_bits):
+def gather(level, proj, wide, depth, sub_bits):
     swap = 2 ** (depth - level - 1)
     bits = [(0, 2**b) for b in range(sub_bits)] + [(2**b, 0) for b in range(depth - level - 1)]
     if level > 0 and len(bits) < 2:
@@ -166,19 +169,20 @@
             for row_mask, sub_mask in [(0, 0)] + bits
         ]
     flip = lax.axis_size("cols") - 1
-    value = exchange(proj, swap, 0, flip)
-    if not bits:
-        return [exchange(value, 0, 0, flip) if flip else value]
+    value = proj
+    own = exchange(wide, 0, 0, flip) if flip else wide
+    cross, step = flip, 0
     while bits:
         now, bits = bits[:2], bits[2:]
         masks = list(now)
         if len(now) == 2:
             masks.append((now[0][0] ^ now[1][0], now[0][1] ^ now[1][1]))
-        terms = [exchange(value, *mask, flip) for mask in masks]
-        terms.append(exchange(value, 0, 0, flip) if flip else value)
-        if bits:
-            value, flip = sum(f32(term) for term in terms), 0
-    return terms
+        terms = [f32(exchange(value, *mask, cross)) for mask in reversed(masks)]
+        own = sum(terms[1:], terms[0]) + f32(own)
+        value, cross = own, 0
+        step += 1
+    total = f32(own)
+    return [exchange(total.astype(jnp.bfloat16), swap, 0, flip)]
 
 
 def per_device(noise, bases, cores, self_mob):
@@ -187,11 +191,11 @@
     size, cols = noise.shape
     count, _, rank = bases.shape
     lanes = 128
-    noise, bases, first = load(noise, bases)
+    noise, bases, first, wide = load(noise, bases)
     parts = []
     for level in range(count):
         proj = project(noise, bases, level) if level else first
-        parts.append(gather(level, proj, depth, sub_bits))
+        parts.append(gather(level, proj, proj if level else wide, depth, sub_bits))
     mixer = pl.pallas_call(
         functools.partial(mixer_kernel, depth),
         out_shape=jax.ShapeDtypeStruct((count, *cores.shape[1:]), cores.dtype),

time: 17.7 us -> 18.2 us (1.028)
  the two profiles are of different devices: /device:TPU:0 before, /device:TPU:1 now
where the time goes in v3:
time: 18.2 us; the launch traced here: 18 us
  starting transfers between devices  10.7 us (59%)
  Pallas kernels  3.85 us (21%)
  waiting for transfers between devices  2.82 us (15%)
  local copies, waits for them, and re-layouts  0.48 us (3%)
    ppermute x7, starting transfers between devices, exchange(): lax.ppermute(value, ('rows', 'sub', 'cols'), [(i, i ^ mask) for i in rang...  10.7 us
    ppermute x7, waiting for transfers between devices, exchange(): lax.ppermute(value, ('rows', 'sub', 'cols'), [(i, i ^ mask) for i in rang...  2.82 us
    pallas_call x1, Pallas kernels, load(): pl.pallas_call(load_kernel, out_shape=(jax.ShapeDtypeStruct(noise.shape,...  1.43 us
    pallas_call x1, Pallas kernels, per_device(): pl.pallas_call(functools.partial(last_kernel, 0), out_shape=shape, in_spe...  1.27 us
    pallas_call x1, Pallas kernels, per_device(): pl.pallas_call(functools.partial(kernel, level), out_shape=shape, in_spec...  0.7 us
    unnamed x4, local copies, waits for them, and re-layouts  0.48 us
  transfers between devices with their start and end apart: 7, of which 2 were waited for; matrix products, arithmetic and copies ran while one was open for 0% of the time, Pallas kernels for 6%

profile of v3, /device:TPU:1, one launch (start us, length us, event | category | flops | bytes accessed | tf_op | source)
XLA Modules:
  0.0 18.0 jit_solution(16192877456255846616)
XLA Ops:
  0.0 1.4 %shard_map.46 = (bf16[1024,128]{1,0:T(8,128)(2,1)S(1)}, bf16[2,1024,256]{2,1,0:T(8,128)(2,1)S(1)}, bf16[128,256]{1,0:T(8,128)(2,1)S(1)}, f32[128,256]{1,0:T(8,128)S(1)}) custom-call(bf16[1024,128]{1,0:T(8,128)(2,1)} %noise_hbm.1, bf16[2,1024,256]{2,1,0:T(8,128)(2,1)} %bases_hbm.1), custom_call_target="tpu_custom_call" | custom-call | flops 67108864 | bytes 1310720 | tf_op jit(solution)/shard_map/pallas_call | solution.py:59
  1.4 0.1 collective-permute-start.5
  1.5 3.7 %collective-permute-start.2 = (bf16[128,256]{1,0:T(8,128)(2,1)S(1)}, bf16[128,256]{1,0:T(8,128)(2,1)S(1)}, u32[]{:S(2)}, u32[]{:S(2)}) collective-permute-start(bf16[128,256]{1,0:T(8,128)(2,1)S(1)} %get-tuple-element.11), channel_id=1, source_target_pairs={{0,7},{1,6},{2,5},{3,4},{4,3},{5,2},{6,1},{7,0},{8,15},{9,14},{10,... | collective-permute-start | bytes 196616 | tf_op jit(solution)/shard_map/ppermute | solution.py:29
  5.2 0.5 %collective-permute-start.3 = (bf16[128,256]{1,0:T(8,128)(2,1)S(1)}, bf16[128,256]{1,0:T(8,128)(2,1)S(1)}, u32[]{:S(2)}, u32[]{:S(2)}) collective-permute-start(bf16[128,256]{1,0:T(8,128)(2,1)S(1)} %get-tuple-element.11), channel_id=1, source_target_pairs={{0,5},{1,4},{2,7},{3,6},{4,1},{5,0},{6,3},{7,2},{8,13},{9,12},{10,... | collective-permute-start | bytes 196616 | tf_op jit(solution)/shard_map/ppermute | solution.py:29
  5.7 0.1 collective-permute-start.4
  5.8 0.3 %shard_map.48 = bf16[128,256]{1,0:T(8,128)(2,1)S(1)} custom-call(bf16[1024,128]{1,0:T(8,128)(2,1)S(1)} %get-tuple-element.9.noise_ref, bf16[2,1024,256]{2,1,0:T(8,128)(2,1)S(1)} %get-tuple-element.10.bases_ref), custom_call_target="tpu_custom_call" | custom-call | flops 67108864 | bytes 786432 | tf_op jit(solution)/shard_map/pallas_call | solution.py:85
  6.1 0.0 copy-start
  6.1 1.5 %collective-permute-start = (bf16[128,256]{1,0:T(8,128)(2,1)S(1)}, bf16[128,256]{1,0:T(8,128)(2,1)S(1)}, u32[]{:S(2)}, u32[]{:S(2)}) collective-permute-start(bf16[128,256]{1,0:T(8,128)(2,1)S(1)} %shard_map.48), channel_id=1, source_target_pairs={{0,4},{1,5},{2,6},{3,7},{4,0},{5,1},{6,2},{7,3},{8,12},{9,13},{10,... | collective-permute-start | bytes 196616 | tf_op jit(solution)/shard_map/ppermute | solution.py:29
  7.5 0.1 collective-permute-done.2
  7.6 2.9 %collective-permute-start.1 = (bf16[128,256]{1,0:T(8,128)(2,1)S(1)}, bf16[128,256]{1,0:T(8,128)(2,1)S(1)}, u32[]{:S(2)}, u32[]{:S(2)}) collective-permute-start(bf16[128,256]{1,0:T(8,128)(2,1)S(1)} %shard_map.48), channel_id=1, source_target_pairs={{0,6},{1,7},{2,4},{3,5},{4,2},{5,3},{6,0},{7,1},{8,14},{9,15},{10,... | collective-permute-start | bytes 196616 | tf_op jit(solution)/shard_map/ppermute | solution.py:29
  10.5 0.0 collective-permute-done.3
  10.5 0.0 collective-permute-done.4
  10.5 0.0 collective-permute-done.5
  10.6 2.0 %collective-permute-start.6 = (bf16[128,256]{1,0:T(8,128)(2,1)S(1)}, bf16[128,256]{1,0:T(8,128)(2,1)S(1)}, u32[]{:S(2)}, u32[]{:S(2)}) collective-permute-start(bf16[128,256]{1,0:T(8,128)(2,1)S(1)} %add_convert_fusion), channel_id=1, source_target_pairs={{0,9},{1,8},{2,11},{3,10},{4,13},{5,12},{6,15},{7,14},{8,1},{9,0},... | collective-permute-start | bytes 196616 | tf_op jit(solution)/shard_map/ppermute | solution.py:29
  12.6 0.0 copy-done
  12.6 0.0 copy-start.1
  12.6 0.2 %shard_map.47.mixer_ref = bf16[2,256,256]{2,1,0:T(8,128)(2,1)S(1)} custom-call(bf16[3,256,256]{2,1,0:T(8,128)(2,1)S(1)} %copy-done), custom_call_target="tpu_custom_call" | custom-call | bytes 786432 | tf_op jit(solution)/shard_map/pallas_call | solution.py:199
  12.8 0.0 collective-permute-done.refs_0_
  12.8 0.0 collective-permute-done.1.refs_1_
  12.8 0.5 %copy-done.1 = f32[1024]{0:T(1024)S(1)} copy-done((f32[1024]{0:T(1024)S(1)}, f32[1024]{0:T(1024)}, u32[]{:S(2)}) %copy-start.1) | copy-done | bytes 4120
  13.3 0.7 %shard_map.49.sum_ref = f32[1024,128]{1,0:T(8,128)S(1)} custom-call(bf16[1024,128]{1,0:T(8,128)(2,1)S(1)} %get-tuple-element.9.noise_ref, f32[8,128]{1,0:T(8,128)S(1)} %bitcast.1, bf16[2,1024,256]{2,1,0:T(8,128)(2,1)S(1)} %get-tuple-element.10.bases_ref, bf16[2,256,256]{2,1,0:T(8,128)(2,1)S(1)} %shard_map.47.mixer_ref, ...), custom_call_target="tpu_custom_call" | custom-call | flops 134217728 | bytes 1048576 | tf_op jit(solution)/shard_map/pallas_call | solution.py:216
  14.0 2.7 %collective-permute-done.6.refs_0_ = bf16[128,256]{1,0:T(8,128)(2,1)S(1)} collective-permute-done((bf16[128,256]{1,0:T(8,128)(2,1)S(1)}, bf16[128,256]{1,0:T(8,128)(2,1)S(1)}, u32[]{:S(2)}, u32[]{:S(2)}) %collective-permute-start.6) | collective-permute-done | bytes 65568 | tf_op jit(solution)/shard_map/ppermute | solution.py:29
  16.7 1.3 %shard_map.50 = f32[1024,128]{1,0:T(8,128)} custom-call(f32[1024,128]{1,0:T(8,128)S(1)} %shard_map.49.sum_ref, bf16[2,1024,256]{2,1,0:T(8,128)(2,1)S(1)} %get-tuple-element.10.bases_ref, bf16[2,256,256]{2,1,0:T(8,128)(2,1)S(1)} %shard_map.47.mixer_ref, bf16[128,256]{1,0:T(8,128)(2,1)S(1)} %collective-permute-done.6.refs_0_), custom_call_target="tpu_custom_call" | custom-call | flops 134217728 | bytes 1048576 | tf_op jit(solution)/shard_map/pallas_call | solution.py:227
  (1 shorter events, 0.0 us)
Async XLA Ops:
  1.4 9.1 %collective-permute-start.5 = (f32[128,256]{1,0:T(8,128)S(1)}, f32[128,256]{1,0:T(8,128)S(1)}, u32[]{:S(2)}, u32[]{:S(2)}) collective-permute-start(f32[128,256]{1,0:T(8,128)S(1)} %get-tuple-element.12), channel_id=1, source_target_pairs={{0,1},{1,0},{2,3},{3,2},{4,5},{5,4},{6,7},{7,6},{8,9},{9,8},{10,11... | collective-permute-start | bytes 393224 | tf_op jit(solution)/shard_map/ppermute | solution.py:29
  1.5 6.1 %collective-permute-start.2 = (bf16[128,256]{1,0:T(8,128)(2,1)S(1)}, bf16[128,256]{1,0:T(8,128)(2,1)S(1)}, u32[]{:S(2)}, u32[]{:S(2)}) collective-permute-start(bf16[128,256]{1,0:T(8,128)(2,1)S(1)} %get-tuple-element.11), channel_id=1, source_target_pairs={{0,7},{1,6},{2,5},{3,4},{4,3},{5,2},{6,1},{7,0},{8,15},{9,14},{10,... | collective-permute-start | bytes 196616 | tf_op jit(solution)/shard_map/ppermute | solution.py:29
  5.2 5.3 %collective-permute-start.3 = (bf16[128,256]{1,0:T(8,128)(2,1)S(1)}, bf16[128,256]{1,0:T(8,128)(2,1)S(1)}, u32[]{:S(2)}, u32[]{:S(2)}) collective-permute-start(bf16[128,256]{1,0:T(8,128)(2,1)S(1)} %get-tuple-element.11), channel_id=1, source_target_pairs={{0,5},{1,4},{2,7},{3,6},{4,1},{5,0},{6,3},{7,2},{8,13},{9,12},{10,... | collective-permute-start | bytes 196616 | tf_op jit(solution)/shard_map/ppermute | solution.py:29
  5.7 4.8 %collective-permute-start.4 = (bf16[128,256]{1,0:T(8,128)(2,1)S(1)}, bf16[128,256]{1,0:T(8,128)(2,1)S(1)}, u32[]{:S(2)}, u32[]{:S(2)}) collective-permute-start(bf16[128,256]{1,0:T(8,128)(2,1)S(1)} %get-tuple-element.11), channel_id=1, source_target_pairs={{0,3},{1,2},{2,1},{3,0},{4,7},{5,6},{6,5},{7,4},{8,11},{9,10},{10,... | collective-permute-start | bytes 196616 | tf_op jit(solution)/shard_map/ppermute | solution.py:29
  6.1 6.5 %copy-start = (bf16[3,256,256]{2,1,0:T(8,128)(2,1)S(1)}, bf16[3,256,256]{2,1,0:T(8,128)(2,1)}, u32[]{:S(2)}) copy-start(bf16[3,256,256]{2,1,0:T(8,128)(2,1)} %cores_ref.1) | copy-start | bytes 1179652
  6.1 6.7 %collective-permute-start = (bf16[128,256]{1,0:T(8,128)(2,1)S(1)}, bf16[128,256]{1,0:T(8,128)(2,1)S(1)}, u32[]{:S(2)}, u32[]{:S(2)}) collective-permute-start(bf16[128,256]{1,0:T(8,128)(2,1)S(1)} %shard_map.48), channel_id=1, source_target_pairs={{0,4},{1,5},{2,6},{3,7},{4,0},{5,1},{6,2},{7,3},{8,12},{9,13},{10,... | collective-permute-start | bytes 196616 | tf_op jit(solution)/shard_map/ppermute | solution.py:29
  7.6 5.2 %collective-permute-start.1 = (bf16[128,256]{1,0:T(8,128)(2,1)S(1)}, bf16[128,256]{1,0:T(8,128)(2,1)S(1)}, u32[]{:S(2)}, u32[]{:S(2)}) collective-permute-start(bf16[128,256]{1,0:T(8,128)(2,1)S(1)} %shard_map.48), channel_id=1, source_target_pairs={{0,6},{1,7},{2,4},{3,5},{4,2},{5,3},{6,0},{7,1},{8,14},{9,15},{10,... | collective-permute-start | bytes 196616 | tf_op jit(solution)/shard_map/ppermute | solution.py:29
  10.6 6.1 %collective-permute-start.6 = (bf16[128,256]{1,0:T(8,128)(2,1)S(1)}, bf16[128,256]{1,0:T(8,128)(2,1)S(1)}, u32[]{:S(2)}, u32[]{:S(2)}) collective-permute-start(bf16[128,256]{1,0:T(8,128)(2,1)S(1)} %add_convert_fusion), channel_id=1, source_target_pairs={{0,9},{1,8},{2,11},{3,10},{4,13},{5,12},{6,15},{7,14},{8,1},{9,0},... | collective-permute-start | bytes 196616 | tf_op jit(solution)/shard_map/ppermute | solution.py:29
  12.6 0.7 %copy-start.1 = (f32[1024]{0:T(1024)S(1)}, f32[1024]{0:T(1024)}, u32[]{:S(2)}) copy-start(f32[1024]{0:T(1024)} %param.7) | copy-start | bytes 12292

commit v4 on v3

--- a/solution.py
+++ b/solution.py
@@ -22,11 +22,13 @@
     return pl.CostEstimate(flops=flops, bytes_accessed=bytes_accessed, transcendentals=0)
 
 
-def exchange(value, row_mask, sub_mask, col_mask):
-    subs, cols = lax.axis_size("sub"), lax.axis_size("cols")
-    count = lax.axis_size("rows") * subs * cols
-    mask = (row_mask * subs + sub_mask) * cols + col_mask
-    return lax.ppermute(value, ("rows", "sub", "cols"), [(i, i ^ mask) for i in range(count)])
+def exchange(value, low_mask, high_mask, col_mask):
+    rows, subs, cols = (lax.axis_size(axis) for axis in ("rows", "sub", "cols"))
+    pairs = []
+    for i in range(rows * subs * cols):
+        row_mask, sub_mask = low_mask if i < rows * subs * cols // 2 else high_mask
+        pairs.append((i, i ^ ((row_mask * subs + sub_mask) * cols + col_mask)))
+    return lax.ppermute(value, ("rows", "sub", "cols"), pairs)
 
 
 def project_onto(noise, basis):
@@ -146,15 +148,27 @@
     out_ref[...] = sum_ref[...] + spread(bases_ref[level], mapped(mixer_ref[level], part_refs))
 
 
-def last_kernel(level, sum_ref, bases_ref, mixer_ref, *refs):
-    part_refs, out_hbm, buf, sems = refs[:-3], refs[-3], refs[-2], refs[-1]
-    weights = mapped(mixer_ref[level], part_refs)
+def fold_kernel(level, bases_ref, mixer_ref, out_ref):
+    rank = bases_ref.shape[2]
+    folded = lax.dot_general(
+        bases_ref[level], mixer_ref[level], (((1,), (1,)), ((), ())), preferred_element_type=jnp.float32
+    )
+    high = folded.astype(jnp.bfloat16)
+    out_ref[:, pl.ds(0, rank)] = high
+    out_ref[:, pl.ds(rank, rank)] = (folded - f32(high)).astype(jnp.bfloat16)
+
+
+def last_kernel(sum_ref, folded_ref, part_ref, out_hbm, buf, sems):
+    part = part_ref[...]
+    both = jnp.concatenate([part, part], axis=1)
     rows = buf.shape[0] // CHUNKS
     copies = []
     for i in range(CHUNKS):
-        part = pl.ds(i * rows, rows)
-        buf[part, :] = sum_ref[part, :] + spread(bases_ref[level, part, :], weights)
-        copies.append(pltpu.make_async_copy(buf.at[part], out_hbm.at[part], sems.at[i]))
+        here = pl.ds(i * rows, rows)
+        buf[here, :] = sum_ref[here, :] + lax.dot_general(
+            folded_ref[here, :], both, (((1,), (1,)), ((), ())), preferred_element_type=jnp.float32
+        )
+        copies.append(pltpu.make_async_copy(buf.at[here], out_hbm.at[here], sems.at[i]))
         copies[-1].start()
     for copy in copies:
         copy.wait()
@@ -164,25 +178,23 @@
     swap = 2 ** (depth - level - 1)
     bits = [(0, 2**b) for b in range(sub_bits)] + [(2**b, 0) for b in range(depth - level - 1)]
     if level > 0 and len(bits) < 2:
-        return [
-            exchange(proj, swap ^ row_mask, sub_mask, 0)
-            for row_mask, sub_mask in [(0, 0)] + bits
-        ]
+        masks = [(swap ^ row_mask, sub_mask) for row_mask, sub_mask in [(0, 0)] + bits]
+        return [exchange(proj, mask, mask, 0) for mask in masks]
     flip = lax.axis_size("cols") - 1
-    value = proj
-    own = exchange(wide, 0, 0, flip) if flip else wide
-    cross, step = flip, 0
+    total = exchange(wide, (0, 0), (0, 0), flip) if flip else wide
+    value, cross, step = proj, flip, 0
     while bits:
         now, bits = bits[:2], bits[2:]
-        masks = list(now)
+        low = high = now
         if len(now) == 2:
-            masks.append((now[0][0] ^ now[1][0], now[0][1] ^ now[1][1]))
-        terms = [f32(exchange(value, *mask, cross)) for mask in reversed(masks)]
-        own = sum(terms[1:], terms[0]) + f32(own)
-        value, cross = own, 0
+            both = (now[0][0] ^ now[1][0], now[0][1] ^ now[1][1])
+            low, high = (both, now[1], now[0]), (now[0], both, now[1])
+        terms = [f32(exchange(value, *masks, cross)) for masks in zip(low, high)]
+        total = sum(terms[1:], terms[0]) + f32(total)
+        value, cross = total, 0
         step += 1
-    total = f32(own)
-    return [exchange(total.astype(jnp.bfloat16), swap, 0, flip)]
+    mask = (swap, 0)
+    return [exchange(f32(total).astype(jnp.bfloat16), mask, mask, flip)]
 
 
 def per_device(noise, bases, cores, self_mob):
@@ -223,9 +235,17 @@
         )(*operands)
     if result is None:
         result = self_mob[:, None] * f32(noise)
-    operands = (result, bases, mixer, *parts[0])
+    folded = pl.pallas_call(
+        functools.partial(fold_kernel, 0),
+        out_shape=jax.ShapeDtypeStruct((size, 2 * rank), jnp.bfloat16),
+        in_specs=[VMEM, VMEM],
+        out_specs=VMEM,
+        compiler_params=PARAMS,
+        cost_estimate=cost(2 * size * rank * rank, size * rank * 6),
+    )(bases, mixer)
+    operands = (result, folded, *parts[0])
     return pl.pallas_call(
-        functools.partial(last_kernel, 0),
+        last_kernel,
         out_shape=shape,
         in_specs=[VMEM] * len(operands),
         out_specs=ANY,

time: 18.2 us -> 17.8 us (0.978)
  starting transfers between devices: 10.7 us -> 10.4 us
    ppermute x7, starting transfers between devices: 10.7 us -> 10.4 us  [exchange(): return lax.ppermute(value, ('rows', 'sub', 'cols'), pairs)]
    pallas_call x1 -> x2, Pallas kernels: 1.27 us -> 1.46 us  [the longest x1 1.13 us: per_device(): pl.pallas_call(last_kernel, out_shape=shape, in_specs=[VMEM] * len(operan...]
  transfers between devices with their start and end apart: 7 -> 7, of which waited for: 2 -> 2; matrix products, arithmetic and copies ran while one was open for 0% -> 0% of each run, Pallas kernels for 6% -> 8%
where the time goes in v4:
time: 17.8 us; the launch traced here: 17.7 us
  starting transfers between devices  10.4 us (58%)
  Pallas kernels  4.03 us (23%)
  waiting for transfers between devices  2.82 us (16%)
  local copies, waits for them, and re-layouts  0.33 us (2%)
    ppermute x7, starting transfers between devices, exchange(): return lax.ppermute(value, ('rows', 'sub', 'cols'), pairs)  10.4 us
    ppermute x7, waiting for transfers between devices, exchange(): return lax.ppermute(value, ('rows', 'sub', 'cols'), pairs)  2.82 us
    pallas_call x1, Pallas kernels, load(): pl.pallas_call(load_kernel, out_shape=(jax.ShapeDtypeStruct(noise.shape,...  1.43 us
    pallas_call x1, Pallas kernels, per_device(): pl.pallas_call(last_kernel, out_shape=shape, in_specs=[VMEM] * len(operan...  1.13 us
    pallas_call x1, Pallas kernels, per_device(): pl.pallas_call(functools.partial(kernel, level), out_shape=shape, in_spec...  0.7 us
  transfers between devices with their start and end apart: 7, of which 2 were waited for; matrix products, arithmetic and copies ran while one was open for 0% of the time, Pallas kernels for 8%

profile of v4, /device:TPU:1, one launch (start us, length us, event | category | flops | bytes accessed | tf_op | source)
XLA Modules:
  0.0 17.7 jit_solution(9166219323101859629)
XLA Ops:
  0.0 1.4 %shard_map.46 = (bf16[1024,128]{1,0:T(8,128)(2,1)S(1)}, bf16[2,1024,256]{2,1,0:T(8,128)(2,1)S(1)}, bf16[128,256]{1,0:T(8,128)(2,1)S(1)}, f32[128,256]{1,0:T(8,128)S(1)}) custom-call(bf16[1024,128]{1,0:T(8,128)(2,1)} %noise_hbm.1, bf16[2,1024,256]{2,1,0:T(8,128)(2,1)} %bases_hbm.1), custom_call_target="tpu_custom_call" | custom-call | flops 67108864 | bytes 1310720 | tf_op jit(solution)/shard_map/pallas_call | solution.py:61
  1.4 0.1 collective-permute-start.5
  1.5 3.7 %collective-permute-start.2 = (bf16[128,256]{1,0:T(8,128)(2,1)S(1)}, bf16[128,256]{1,0:T(8,128)(2,1)S(1)}, u32[]{:S(2)}, u32[]{:S(2)}) collective-permute-start(bf16[128,256]{1,0:T(8,128)(2,1)S(1)} %get-tuple-element.11), channel_id=1, source_target_pairs={{0,7},{1,6},{2,5},{3,4},{4,3},{5,2},{6,1},{7,0},{8,11},{9,10},{10,... | collective-permute-start | bytes 196616 | tf_op jit(solution)/shard_map/ppermute | solution.py:31
  5.2 0.5 %collective-permute-start.3 = (bf16[128,256]{1,0:T(8,128)(2,1)S(1)}, bf16[128,256]{1,0:T(8,128)(2,1)S(1)}, u32[]{:S(2)}, u32[]{:S(2)}) collective-permute-start(bf16[128,256]{1,0:T(8,128)(2,1)S(1)} %get-tuple-element.11), channel_id=1, source_target_pairs={{0,5},{1,4},{2,7},{3,6},{4,1},{5,0},{6,3},{7,2},{8,15},{9,14},{10,... | collective-permute-start | bytes 196616 | tf_op jit(solution)/shard_map/ppermute | solution.py:31
  5.7 0.1 collective-permute-start.4
  5.8 0.3 %shard_map.48 = bf16[128,256]{1,0:T(8,128)(2,1)S(1)} custom-call(bf16[1024,128]{1,0:T(8,128)(2,1)S(1)} %get-tuple-element.9.noise_ref, bf16[2,1024,256]{2,1,0:T(8,128)(2,1)S(1)} %get-tuple-element.10.bases_ref), custom_call_target="tpu_custom_call" | custom-call | flops 67108864 | bytes 786432 | tf_op jit(solution)/shard_map/pallas_call | solution.py:87
  6.1 0.0 copy-start
  6.1 1.5 %collective-permute-start = (bf16[128,256]{1,0:T(8,128)(2,1)S(1)}, bf16[128,256]{1,0:T(8,128)(2,1)S(1)}, u32[]{:S(2)}, u32[]{:S(2)}) collective-permute-start(bf16[128,256]{1,0:T(8,128)(2,1)S(1)} %shard_map.48), channel_id=1, source_target_pairs={{0,4},{1,5},{2,6},{3,7},{4,0},{5,1},{6,2},{7,3},{8,12},{9,13},{10,... | collective-permute-start | bytes 196616 | tf_op jit(solution)/shard_map/ppermute | solution.py:31
  7.5 0.1 collective-permute-done.2
  7.6 2.9 %collective-permute-start.1 = (bf16[128,256]{1,0:T(8,128)(2,1)S(1)}, bf16[128,256]{1,0:T(8,128)(2,1)S(1)}, u32[]{:S(2)}, u32[]{:S(2)}) collective-permute-start(bf16[128,256]{1,0:T(8,128)(2,1)S(1)} %shard_map.48), channel_id=1, source_target_pairs={{0,6},{1,7},{2,4},{3,5},{4,2},{5,3},{6,0},{7,1},{8,14},{9,15},{10,... | collective-permute-start | bytes 196616 | tf_op jit(solution)/shard_map/ppermute | solution.py:31
  10.5 0.0 collective-permute-done.3
  10.5 0.0 collective-permute-done.4
  10.5 0.0 collective-permute-done.5
  10.6 1.6 %collective-permute-start.6 = (bf16[128,256]{1,0:T(8,128)(2,1)S(1)}, bf16[128,256]{1,0:T(8,128)(2,1)S(1)}, u32[]{:S(2)}, u32[]{:S(2)}) collective-permute-start(bf16[128,256]{1,0:T(8,128)(2,1)S(1)} %add_convert_fusion), channel_id=1, source_target_pairs={{0,9},{1,8},{2,11},{3,10},{4,13},{5,12},{6,15},{7,14},{8,1},{9,0},... | collective-permute-start | bytes 196616 | tf_op jit(solution)/shard_map/ppermute | solution.py:31
  12.2 0.0 copy-done
  12.2 0.2 %shard_map.47.mixer_ref = bf16[2,256,256]{2,1,0:T(8,128)(2,1)S(1)} custom-call(bf16[3,256,256]{2,1,0:T(8,128)(2,1)S(1)} %copy-done), custom_call_target="tpu_custom_call" | custom-call | bytes 786432 | tf_op jit(solution)/shard_map/pallas_call | solution.py:211
  12.4 0.0 copy-start.1
  12.4 0.3 %shard_map.50.folded_ref = bf16[1024,512]{1,0:T(8,128)(2,1)S(1)} custom-call(bf16[2,1024,256]{2,1,0:T(8,128)(2,1)S(1)} %get-tuple-element.10.bases_ref, bf16[2,256,256]{2,1,0:T(8,128)(2,1)S(1)} %shard_map.47.mixer_ref), custom_call_target="tpu_custom_call" | custom-call | flops 134217728 | bytes 1572864 | tf_op jit(solution)/shard_map/pallas_call | solution.py:238
  12.7 0.0 collective-permute-done.refs_0_
  12.7 0.0 collective-permute-done.1.refs_1_
  12.8 0.3 %copy-done.1 = f32[1024]{0:T(1024)S(1)} copy-done((f32[1024]{0:T(1024)S(1)}, f32[1024]{0:T(1024)}, u32[]{:S(2)}) %copy-start.1) | copy-done | bytes 4120
  13.1 0.7 %shard_map.49.sum_ref = f32[1024,128]{1,0:T(8,128)S(1)} custom-call(bf16[1024,128]{1,0:T(8,128)(2,1)S(1)} %get-tuple-element.9.noise_ref, f32[8,128]{1,0:T(8,128)S(1)} %bitcast.1, bf16[2,1024,256]{2,1,0:T(8,128)(2,1)S(1)} %get-tuple-element.10.bases_ref, bf16[2,256,256]{2,1,0:T(8,128)(2,1)S(1)} %shard_map.47.mixer_ref, ...), custom_call_target="tpu_custom_call" | custom-call | flops 134217728 | bytes 1048576 | tf_op jit(solution)/shard_map/pallas_call | solution.py:228
  13.8 2.7 %collective-permute-done.6.part_ref = bf16[128,256]{1,0:T(8,128)(2,1)S(1)} collective-permute-done((bf16[128,256]{1,0:T(8,128)(2,1)S(1)}, bf16[128,256]{1,0:T(8,128)(2,1)S(1)}, u32[]{:S(2)}, u32[]{:S(2)}) %collective-permute-start.6) | collective-permute-done | bytes 65568 | tf_op jit(solution)/shard_map/ppermute | solution.py:31
  16.5 1.1 %shard_map.51 = f32[1024,128]{1,0:T(8,128)} custom-call(f32[1024,128]{1,0:T(8,128)S(1)} %shard_map.49.sum_ref, bf16[1024,512]{1,0:T(8,128)(2,1)S(1)} %shard_map.50.folded_ref, bf16[128,256]{1,0:T(8,128)(2,1)S(1)} %collective-permute-done.6.part_ref), custom_call_target="tpu_custom_call" | custom-call | flops 134217728 | bytes 1048576 | tf_op jit(solution)/shard_map/pallas_call | solution.py:247
  (1 shorter events, 0.0 us)
Async XLA Ops:
  1.4 9.1 %collective-permute-start.5 = (f32[128,256]{1,0:T(8,128)S(1)}, f32[128,256]{1,0:T(8,128)S(1)}, u32[]{:S(2)}, u32[]{:S(2)}) collective-permute-start(f32[128,256]{1,0:T(8,128)S(1)} %get-tuple-element.12), channel_id=1, source_target_pairs={{0,1},{1,0},{2,3},{3,2},{4,5},{5,4},{6,7},{7,6},{8,9},{9,8},{10,11... | collective-permute-start | bytes 393224 | tf_op jit(solution)/shard_map/ppermute | solution.py:31
  1.5 6.1 %collective-permute-start.2 = (bf16[128,256]{1,0:T(8,128)(2,1)S(1)}, bf16[128,256]{1,0:T(8,128)(2,1)S(1)}, u32[]{:S(2)}, u32[]{:S(2)}) collective-permute-start(bf16[128,256]{1,0:T(8,128)(2,1)S(1)} %get-tuple-element.11), channel_id=1, source_target_pairs={{0,7},{1,6},{2,5},{3,4},{4,3},{5,2},{6,1},{7,0},{8,11},{9,10},{10,... | collective-permute-start | bytes 196616 | tf_op jit(solution)/shard_map/ppermute | solution.py:31
  5.2 5.3 %collective-permute-start.3 = (bf16[128,256]{1,0:T(8,128)(2,1)S(1)}, bf16[128,256]{1,0:T(8,128)(2,1)S(1)}, u32[]{:S(2)}, u32[]{:S(2)}) collective-permute-start(bf16[128,256]{1,0:T(8,128)(2,1)S(1)} %get-tuple-element.11), channel_id=1, source_target_pairs={{0,5},{1,4},{2,7},{3,6},{4,1},{5,0},{6,3},{7,2},{8,15},{9,14},{10,... | collective-permute-start | bytes 196616 | tf_op jit(solution)/shard_map/ppermute | solution.py:31
  5.7 4.8 %collective-permute-start.4 = (bf16[128,256]{1,0:T(8,128)(2,1)S(1)}, bf16[128,256]{1,0:T(8,128)(2,1)S(1)}, u32[]{:S(2)}, u32[]{:S(2)}) collective-permute-start(bf16[128,256]{1,0:T(8,128)(2,1)S(1)} %get-tuple-element.11), channel_id=1, source_target_pairs={{0,3},{1,2},{2,1},{3,0},{4,7},{5,6},{6,5},{7,4},{8,13},{9,12},{10,... | collective-permute-start | bytes 196616 | tf_op jit(solution)/shard_map/ppermute | solution.py:31
  6.1 6.1 %copy-start = (bf16[3,256,256]{2,1,0:T(8,128)(2,1)S(1)}, bf16[3,256,256]{2,1,0:T(8,128)(2,1)}, u32[]{:S(2)}) copy-start(bf16[3,256,256]{2,1,0:T(8,128)(2,1)} %cores_ref.1) | copy-start | bytes 1179652
  6.1 6.7 %collective-permute-start = (bf16[128,256]{1,0:T(8,128)(2,1)S(1)}, bf16[128,256]{1,0:T(8,128)(2,1)S(1)}, u32[]{:S(2)}, u32[]{:S(2)}) collective-permute-start(bf16[128,256]{1,0:T(8,128)(2,1)S(1)} %shard_map.48), channel_id=1, source_target_pairs={{0,4},{1,5},{2,6},{3,7},{4,0},{5,1},{6,2},{7,3},{8,12},{9,13},{10,... | collective-permute-start | bytes 196616 | tf_op jit(solution)/shard_map/ppermute | solution.py:31
  7.6 5.1 %collective-permute-start.1 = (bf16[128,256]{1,0:T(8,128)(2,1)S(1)}, bf16[128,256]{1,0:T(8,128)(2,1)S(1)}, u32[]{:S(2)}, u32[]{:S(2)}) collective-permute-start(bf16[128,256]{1,0:T(8,128)(2,1)S(1)} %shard_map.48), channel_id=1, source_target_pairs={{0,6},{1,7},{2,4},{3,5},{4,2},{5,3},{6,0},{7,1},{8,14},{9,15},{10,... | collective-permute-start | bytes 196616 | tf_op jit(solution)/shard_map/ppermute | solution.py:31
  10.6 6.0 %collective-permute-start.6 = (bf16[128,256]{1,0:T(8,128)(2,1)S(1)}, bf16[128,256]{1,0:T(8,128)(2,1)S(1)}, u32[]{:S(2)}, u32[]{:S(2)}) collective-permute-start(bf16[128,256]{1,0:T(8,128)(2,1)S(1)} %add_convert_fusion), channel_id=1, source_target_pairs={{0,9},{1,8},{2,11},{3,10},{4,13},{5,12},{6,15},{7,14},{8,1},{9,0},... | collective-permute-start | bytes 196616 | tf_op jit(solution)/shard_map/ppermute | solution.py:31
  12.4 0.7 %copy-start.1 = (f32[1024]{0:T(1024)S(1)}, f32[1024]{0:T(1024)}, u32[]{:S(2)}) copy-start(f32[1024]{0:T(1024)} %param.7) | copy-start | bytes 12292

commit v5 on v4

--- a/solution.py
+++ b/solution.py
@@ -22,11 +22,12 @@
     return pl.CostEstimate(flops=flops, bytes_accessed=bytes_accessed, transcendentals=0)
 
 
-def exchange(value, low_mask, high_mask, col_mask):
+def exchange(value, low_mask, high_mask, col_mask, odd_mask=None):
     rows, subs, cols = (lax.axis_size(axis) for axis in ("rows", "sub", "cols"))
     pairs = []
     for i in range(rows * subs * cols):
-        row_mask, sub_mask = low_mask if i < rows * subs * cols // 2 else high_mask
+        low, odd = i < rows * subs * cols // 2, i // cols % subs % 2
+        row_mask, sub_mask = low_mask if low else odd_mask if odd and odd_mask else high_mask
         pairs.append((i, i ^ ((row_mask * subs + sub_mask) * cols + col_mask)))
     return lax.ppermute(value, ("rows", "sub", "cols"), pairs)
 
@@ -47,8 +48,9 @@
     for copy in copies:
         copy.start()
     copies[0].wait()
+    turned = noise_ref[...].T
     copies[1].wait()
-    proj = project_onto(noise_ref[...], bases_ref[0])
+    proj = jnp.dot(turned, bases_ref[0], preferred_element_type=jnp.float32)
     out_ref[...] = proj.astype(out_ref.dtype)
     wide_ref[...] = proj
     for copy in copies[2:]:
@@ -193,8 +195,8 @@
         total = sum(terms[1:], terms[0]) + f32(total)
         value, cross = total, 0
         step += 1
-    mask = (swap, 0)
-    return [exchange(f32(total).astype(jnp.bfloat16), mask, mask, flip)]
+    mask, odd_mask = (swap, 0), (swap + swap // 2, 0)
+    return [exchange(f32(total).astype(jnp.bfloat16), mask, mask, flip, odd_mask)]
 
 
 def per_device(noise, bases, cores, self_mob):

time: 17.8 us -> 17.8 us (level)
  no operation moved by 1% of the time
where the time goes in v5:
time: 17.8 us; the launch traced here: 17.6 us
  starting transfers between devices  10.3 us (58%)
  Pallas kernels  3.99 us (22%)
  waiting for transfers between devices  2.82 us (16%)
  local copies, waits for them, and re-layouts  0.32 us (2%)
    ppermute x7, starting transfers between devices, exchange(): return lax.ppermute(value, ('rows', 'sub', 'cols'), pairs)  10.3 us
    ppermute x7, waiting for transfers between devices, exchange(): return lax.ppermute(value, ('rows', 'sub', 'cols'), pairs)  2.82 us
    pallas_call x1, Pallas kernels, load(): pl.pallas_call(load_kernel, out_shape=(jax.ShapeDtypeStruct(noise.shape,...  1.39 us
    pallas_call x1, Pallas kernels, per_device(): pl.pallas_call(last_kernel, out_shape=shape, in_specs=[VMEM] * len(operan...  1.12 us
    pallas_call x1, Pallas kernels, per_device(): pl.pallas_call(functools.partial(kernel, level), out_shape=shape, in_spec...  0.7 us
  transfers between devices with their start and end apart: 7, of which 2 were waited for; matrix products, arithmetic and copies ran while one was open for 0% of the time, Pallas kernels for 8%

profile of v5, /device:TPU:1, one launch (start us, length us, event | category | flops | bytes accessed | tf_op | source)
XLA Modules:
  0.0 17.6 jit_solution(12634061241333256940)
XLA Ops:
  0.0 1.4 %shard_map.46 = (bf16[1024,128]{1,0:T(8,128)(2,1)S(1)}, bf16[2,1024,256]{2,1,0:T(8,128)(2,1)S(1)}, bf16[128,256]{1,0:T(8,128)(2,1)S(1)}, f32[128,256]{1,0:T(8,128)S(1)}) custom-call(bf16[1024,128]{1,0:T(8,128)(2,1)} %noise_hbm.1, bf16[2,1024,256]{2,1,0:T(8,128)(2,1)} %bases_hbm.1), custom_call_target="tpu_custom_call" | custom-call | flops 67108864 | bytes 1310720 | tf_op jit(solution)/shard_map/pallas_call | solution.py:63
  1.4 0.1 collective-permute-start.5
  1.5 3.7 %collective-permute-start.2 = (bf16[128,256]{1,0:T(8,128)(2,1)S(1)}, bf16[128,256]{1,0:T(8,128)(2,1)S(1)}, u32[]{:S(2)}, u32[]{:S(2)}) collective-permute-start(bf16[128,256]{1,0:T(8,128)(2,1)S(1)} %get-tuple-element.11), channel_id=1, source_target_pairs={{0,7},{1,6},{2,5},{3,4},{4,3},{5,2},{6,1},{7,0},{8,11},{9,10},{10,... | collective-permute-start | bytes 196616 | tf_op jit(solution)/shard_map/ppermute | solution.py:32
  5.1 0.5 %collective-permute-start.3 = (bf16[128,256]{1,0:T(8,128)(2,1)S(1)}, bf16[128,256]{1,0:T(8,128)(2,1)S(1)}, u32[]{:S(2)}, u32[]{:S(2)}) collective-permute-start(bf16[128,256]{1,0:T(8,128)(2,1)S(1)} %get-tuple-element.11), channel_id=1, source_target_pairs={{0,5},{1,4},{2,7},{3,6},{4,1},{5,0},{6,3},{7,2},{8,15},{9,14},{10,... | collective-permute-start | bytes 196616 | tf_op jit(solution)/shard_map/ppermute | solution.py:32
  5.6 0.1 collective-permute-start.4
  5.7 0.3 %shard_map.48 = bf16[128,256]{1,0:T(8,128)(2,1)S(1)} custom-call(bf16[1024,128]{1,0:T(8,128)(2,1)S(1)} %get-tuple-element.9.noise_ref, bf16[2,1024,256]{2,1,0:T(8,128)(2,1)S(1)} %get-tuple-element.10.bases_ref), custom_call_target="tpu_custom_call" | custom-call | flops 67108864 | bytes 786432 | tf_op jit(solution)/shard_map/pallas_call | solution.py:89
  6.0 0.0 copy-start
  6.0 1.5 %collective-permute-start = (bf16[128,256]{1,0:T(8,128)(2,1)S(1)}, bf16[128,256]{1,0:T(8,128)(2,1)S(1)}, u32[]{:S(2)}, u32[]{:S(2)}) collective-permute-start(bf16[128,256]{1,0:T(8,128)(2,1)S(1)} %shard_map.48), channel_id=1, source_target_pairs={{0,4},{1,5},{2,6},{3,7},{4,0},{5,1},{6,2},{7,3},{8,12},{9,13},{10,... | collective-permute-start | bytes 196616 | tf_op jit(solution)/shard_map/ppermute | solution.py:32
  7.5 0.1 collective-permute-done.2
  7.6 2.9 %collective-permute-start.1 = (bf16[128,256]{1,0:T(8,128)(2,1)S(1)}, bf16[128,256]{1,0:T(8,128)(2,1)S(1)}, u32[]{:S(2)}, u32[]{:S(2)}) collective-permute-start(bf16[128,256]{1,0:T(8,128)(2,1)S(1)} %shard_map.48), channel_id=1, source_target_pairs={{0,6},{1,7},{2,4},{3,5},{4,2},{5,3},{6,0},{7,1},{8,14},{9,15},{10,... | collective-permute-start | bytes 196616 | tf_op jit(solution)/shard_map/ppermute | solution.py:32
  10.5 0.0 collective-permute-done.3
  10.5 0.0 collective-permute-done.4
  10.5 0.0 collective-permute-done.5
  10.5 1.6 %collective-permute-start.6 = (bf16[128,256]{1,0:T(8,128)(2,1)S(1)}, bf16[128,256]{1,0:T(8,128)(2,1)S(1)}, u32[]{:S(2)}, u32[]{:S(2)}) collective-permute-start(bf16[128,256]{1,0:T(8,128)(2,1)S(1)} %add_convert_fusion), channel_id=1, source_target_pairs={{0,9},{1,8},{2,11},{3,10},{4,13},{5,12},{6,15},{7,14},{8,1},{9,0},... | collective-permute-start | bytes 196616 | tf_op jit(solution)/shard_map/ppermute | solution.py:32
  12.1 0.0 copy-done
  12.1 0.2 %shard_map.47.mixer_ref = bf16[2,256,256]{2,1,0:T(8,128)(2,1)S(1)} custom-call(bf16[3,256,256]{2,1,0:T(8,128)(2,1)S(1)} %copy-done), custom_call_target="tpu_custom_call" | custom-call | bytes 786432 | tf_op jit(solution)/shard_map/pallas_call | solution.py:213
  12.3 0.0 copy-start.1
  12.3 0.3 %shard_map.50.folded_ref = bf16[1024,512]{1,0:T(8,128)(2,1)S(1)} custom-call(bf16[2,1024,256]{2,1,0:T(8,128)(2,1)S(1)} %get-tuple-element.10.bases_ref, bf16[2,256,256]{2,1,0:T(8,128)(2,1)S(1)} %shard_map.47.mixer_ref), custom_call_target="tpu_custom_call" | custom-call | flops 134217728 | bytes 1572864 | tf_op jit(solution)/shard_map/pallas_call | solution.py:240
  12.7 0.0 collective-permute-done.refs_0_
  12.7 0.0 collective-permute-done.1.refs_1_
  12.7 0.3 %copy-done.1 = f32[1024]{0:T(1024)S(1)} copy-done((f32[1024]{0:T(1024)S(1)}, f32[1024]{0:T(1024)}, u32[]{:S(2)}) %copy-start.1) | copy-done | bytes 4120
  13.0 0.7 %shard_map.49.sum_ref = f32[1024,128]{1,0:T(8,128)S(1)} custom-call(bf16[1024,128]{1,0:T(8,128)(2,1)S(1)} %get-tuple-element.9.noise_ref, f32[8,128]{1,0:T(8,128)S(1)} %bitcast.1, bf16[2,1024,256]{2,1,0:T(8,128)(2,1)S(1)} %get-tuple-element.10.bases_ref, bf16[2,256,256]{2,1,0:T(8,128)(2,1)S(1)} %shard_map.47.mixer_ref, ...), custom_call_target="tpu_custom_call" | custom-call | flops 134217728 | bytes 1048576 | tf_op jit(solution)/shard_map/pallas_call | solution.py:230
  13.7 2.7 %collective-permute-done.6.part_ref = bf16[128,256]{1,0:T(8,128)(2,1)S(1)} collective-permute-done((bf16[128,256]{1,0:T(8,128)(2,1)S(1)}, bf16[128,256]{1,0:T(8,128)(2,1)S(1)}, u32[]{:S(2)}, u32[]{:S(2)}) %collective-permute-start.6) | collective-permute-done | bytes 65568 | tf_op jit(solution)/shard_map/ppermute | solution.py:32
  16.5 1.1 %shard_map.51 = f32[1024,128]{1,0:T(8,128)} custom-call(f32[1024,128]{1,0:T(8,128)S(1)} %shard_map.49.sum_ref, bf16[1024,512]{1,0:T(8,128)(2,1)S(1)} %shard_map.50.folded_ref, bf16[128,256]{1,0:T(8,128)(2,1)S(1)} %collective-permute-done.6.part_ref), custom_call_target="tpu_custom_call" | custom-call | flops 134217728 | bytes 1048576 | tf_op jit(solution)/shard_map/pallas_call | solution.py:249
  (1 shorter events, 0.0 us)
Async XLA Ops:
  1.4 9.1 %collective-permute-start.5 = (f32[128,256]{1,0:T(8,128)S(1)}, f32[128,256]{1,0:T(8,128)S(1)}, u32[]{:S(2)}, u32[]{:S(2)}) collective-permute-start(f32[128,256]{1,0:T(8,128)S(1)} %get-tuple-element.12), channel_id=1, source_target_pairs={{0,1},{1,0},{2,3},{3,2},{4,5},{5,4},{6,7},{7,6},{8,9},{9,8},{10,11... | collective-permute-start | bytes 393224 | tf_op jit(solution)/shard_map/ppermute | solution.py:32
  1.5 6.1 %collective-permute-start.2 = (bf16[128,256]{1,0:T(8,128)(2,1)S(1)}, bf16[128,256]{1,0:T(8,128)(2,1)S(1)}, u32[]{:S(2)}, u32[]{:S(2)}) collective-permute-start(bf16[128,256]{1,0:T(8,128)(2,1)S(1)} %get-tuple-element.11), channel_id=1, source_target_pairs={{0,7},{1,6},{2,5},{3,4},{4,3},{5,2},{6,1},{7,0},{8,11},{9,10},{10,... | collective-permute-start | bytes 196616 | tf_op jit(solution)/shard_map/ppermute | solution.py:32
  5.1 5.3 %collective-permute-start.3 = (bf16[128,256]{1,0:T(8,128)(2,1)S(1)}, bf16[128,256]{1,0:T(8,128)(2,1)S(1)}, u32[]{:S(2)}, u32[]{:S(2)}) collective-permute-start(bf16[128,256]{1,0:T(8,128)(2,1)S(1)} %get-tuple-element.11), channel_id=1, source_target_pairs={{0,5},{1,4},{2,7},{3,6},{4,1},{5,0},{6,3},{7,2},{8,15},{9,14},{10,... | collective-permute-start | bytes 196616 | tf_op jit(solution)/shard_map/ppermute | solution.py:32
  5.6 4.8 %collective-permute-start.4 = (bf16[128,256]{1,0:T(8,128)(2,1)S(1)}, bf16[128,256]{1,0:T(8,128)(2,1)S(1)}, u32[]{:S(2)}, u32[]{:S(2)}) collective-permute-start(bf16[128,256]{1,0:T(8,128)(2,1)S(1)} %get-tuple-element.11), channel_id=1, source_target_pairs={{0,3},{1,2},{2,1},{3,0},{4,7},{5,6},{6,5},{7,4},{8,13},{9,12},{10,... | collective-permute-start | bytes 196616 | tf_op jit(solution)/shard_map/ppermute | solution.py:32
  6.0 6.1 %copy-start = (bf16[3,256,256]{2,1,0:T(8,128)(2,1)S(1)}, bf16[3,256,256]{2,1,0:T(8,128)(2,1)}, u32[]{:S(2)}) copy-start(bf16[3,256,256]{2,1,0:T(8,128)(2,1)} %cores_ref.1) | copy-start | bytes 1179652
  6.0 6.7 %collective-permute-start = (bf16[128,256]{1,0:T(8,128)(2,1)S(1)}, bf16[128,256]{1,0:T(8,128)(2,1)S(1)}, u32[]{:S(2)}, u32[]{:S(2)}) collective-permute-start(bf16[128,256]{1,0:T(8,128)(2,1)S(1)} %shard_map.48), channel_id=1, source_target_pairs={{0,4},{1,5},{2,6},{3,7},{4,0},{5,1},{6,2},{7,3},{8,12},{9,13},{10,... | collective-permute-start | bytes 196616 | tf_op jit(solution)/shard_map/ppermute | solution.py:32
  7.6 5.1 %collective-permute-start.1 = (bf16[128,256]{1,0:T(8,128)(2,1)S(1)}, bf16[128,256]{1,0:T(8,128)(2,1)S(1)}, u32[]{:S(2)}, u32[]{:S(2)}) collective-permute-start(bf16[128,256]{1,0:T(8,128)(2,1)S(1)} %shard_map.48), channel_id=1, source_target_pairs={{0,6},{1,7},{2,4},{3,5},{4,2},{5,3},{6,0},{7,1},{8,14},{9,15},{10,... | collective-permute-start | bytes 196616 | tf_op jit(solution)/shard_map/ppermute | solution.py:32
  10.5 5.9 %collective-permute-start.6 = (bf16[128,256]{1,0:T(8,128)(2,1)S(1)}, bf16[128,256]{1,0:T(8,128)(2,1)S(1)}, u32[]{:S(2)}, u32[]{:S(2)}) collective-permute-start(bf16[128,256]{1,0:T(8,128)(2,1)S(1)} %add_convert_fusion), channel_id=1, source_target_pairs={{0,9},{1,8},{2,11},{3,10},{4,13},{5,12},{6,15},{7,14},{8,1},{9,0},... | collective-permute-start | bytes 196616 | tf_op jit(solution)/shard_map/ppermute | solution.py:32
  12.3 0.7 %copy-start.1 = (f32[1024]{0:T(1024)S(1)}, f32[1024]{0:T(1024)}, u32[]{:S(2)}) copy-start(f32[1024]{0:T(1024)} %param.7) | copy-start | bytes 12292
